TPU v7x, 32 devices: a whole 2x2x4 slice. The times are simulated.
32 devices in a mesh: mode: 8 (over y, x, core), space: 4 (over z).
Axes of the slice: x: 2, y: 2, z: 4, core: 2. Of those that a mesh axis runs over, the one named last changes fastest.
Arguments:
- left_modes: bfloat16 [512, 24, 512], P('mode', None, 'space'), may hold values from -6 to 6
- right_modes: bfloat16 [512, 24, 512], P('mode', None, 'space'), may hold values from -6 to 6
- momenta: int32 [8, 3], replicated, may hold values from -3 to 3
- spin_perm: int32 [8, 4], replicated, may hold values from 0 to 3, each once within a row
- spin_phase: int32 [8, 4], replicated, may hold values from 0 to 3
Outputs:
- fields: float32 [64, 512, 64], P('space', 'mode')
Inputs may be any that keep to these rules, and one draw needn't show every extreme that they name: `spin_perm`: each row is a permutation of 0 to 3.
All inputs are finite; a program needn't handle non-finite values.
Results may differ from a plain program's by a relative error of at most 0.0028.
Values may be sent and summed in bfloat16 or wider, within the bound.
No kernel may reach another device: no remote copies, remote signals or barrier semaphores. Data moves between devices by JAX's collectives and lax.ppermute only.
A program may use at most 64 MiB of HBM per device.

v0:
```python
import math

import jax
import jax.numpy as jnp
from jax import lax
from jax.sharding import PartitionSpec as P

STRUCTS = 8
CYCLE = 4
LAT = 96
BOX = 16


def from_behind(block, axis, distance):
    devices = range(lax.axis_size(axis))
    route = [((i - distance) % len(devices), i) for i in devices]
    return lax.ppermute(block, axis, route)


def turned_rows(mode_rows, momenta, spin_perm, spin_phase, coords, struct_id):
    mode_count = mode_rows.shape[0]
    site_count = mode_rows.shape[2]
    real_part = mode_rows[:, :12, :].astype(jnp.float32).reshape(mode_count, 4, 3, site_count)
    imag_part = mode_rows[:, 12:, :].astype(jnp.float32).reshape(mode_count, 4, 3, site_count)
    momentum_dot = jnp.sum(momenta[struct_id][:, None] * coords, axis=0)
    quarter = jnp.mod(LAT // 4 * spin_phase[struct_id][:, None] - momentum_dot[None, :], LAT)
    phase_angle = quarter.astype(jnp.float32) * (2.0 * math.pi / LAT)
    cosine = jnp.cos(phase_angle)[None, :, None, :]
    sine_val = jnp.sin(phase_angle)[None, :, None, :]
    turn_re = real_part * cosine + imag_part * sine_val
    turn_im = imag_part * cosine - real_part * sine_val
    chooser = (spin_perm[struct_id][:, None] == jnp.arange(4, dtype=jnp.int32)[None, :]).astype(
        jnp.float32
    )
    moved_re = chooser[0][None, :, None, None] * turn_re[:, 0:1]
    moved_im = chooser[0][None, :, None, None] * turn_im[:, 0:1]
    for spin_from in range(1, 4):
        moved_re = (
            moved_re
            + chooser[spin_from][None, :, None, None] * turn_re[:, spin_from : spin_from + 1]
        )
        moved_im = (
            moved_im
            + chooser[spin_from][None, :, None, None] * turn_im[:, spin_from : spin_from + 1]
        )
    re_rows = jnp.concatenate([moved_re, moved_im], axis=1).reshape(mode_count, 24, site_count)
    im_rows = jnp.concatenate([-moved_im, moved_re], axis=1).reshape(mode_count, 24, site_count)
    stacked = jnp.stack([re_rows, im_rows]).astype(jnp.bfloat16)
    return stacked.reshape(2 * mode_count, 24 * site_count)


def local(left_modes, right_modes, momenta, spin_perm, spin_phase):
    mode_count, comp_count, site_count = left_modes.shape
    space_count = lax.axis_size("space")
    site_index = lax.axis_index("space") * site_count + lax.iota(jnp.int32, site_count)
    coords = jnp.stack([site_index % BOX, site_index // BOX % BOX, site_index // (BOX * BOX)])
    blocks = [right_modes]
    current = right_modes
    for shift_step in range(1, CYCLE):
        current = from_behind(current, "mode", 1)
        blocks.append(current)
    rights = jnp.stack(blocks).reshape(CYCLE * mode_count, comp_count * site_count)
    all_rows = jnp.concatenate(
        [
            turned_rows(left_modes, momenta, spin_perm, spin_phase, coords, struct_id)
            for struct_id in range(STRUCTS)
        ],
        axis=0,
    )
    product = lax.dot_general(
        all_rows, rights, (((1,), (1,)), ((), ())), preferred_element_type=jnp.float32
    )
    partial_value = product.reshape(STRUCTS, 2, mode_count, CYCLE, mode_count).transpose(
        0, 3, 1, 2, 4
    )
    partial_value = partial_value.reshape(STRUCTS * CYCLE * 2, mode_count, mode_count)
    owned = lax.psum_scatter(partial_value, "space", scatter_dimension=0, tiled=True)
    factor = 1.0 / math.sqrt(24 * site_count * space_count)
    return owned * factor


def solution(mesh):
    placed = (P("mode", None, "space"), P("mode", None, "space"), P(), P(), P())
    return jax.shard_map(
        local, mesh=mesh, in_specs=placed, out_specs=P("space", "mode", None), check_vma=False
    )
```

profile of v0, /device:TPU:0, one launch (start us, length us, event | category | flops | bytes accessed | tf_op | source)
XLA Modules:
  0.0 106.6 jit_solution(6042522122504200473)
XLA Ops:
  7.1 1.2 %stack.62 = bf16[1,64,3072]{2,1,0:T(8,128)(2,1)S(1)} reshape(bf16[64,24,128]{2,1,0:T(8,128)(2,1)} %param.6) | data formatting | bytes 786432 | tf_op jit(solution)/shard_map/stack | solution.py:62
  8.2 1.3 %slice_reduce_fusion = (s32[3]{0:T(128)S(1)}, s32[3]{0:T(128)S(1)}, s32[3]{0:T(128)S(1)}, s32[3]{0:T(128)S(1)}, s32[3]{0:T(128)S(1)}, /*index=5*/s32[3]{0:T(128)S(1)}, s32[3]{0:T(128)S(1)}, s32[3]{0:T(128)S(1)}) fusion(s32[8,3]{0,1:T(4,128)} %param.7), kind=kLoop, calls=%fused_computation.216 | loop fusion | bytes 192 | tf_op jit(solution)/shard_map/slice | solution.py:25
  9.5 1.3 %multiply_reduce_fusion.1 = (s32[4]{0:T(128)S(1)}, s32[4]{0:T(128)S(1)}, s32[4]{0:T(128)S(1)}, s32[4]{0:T(128)S(1)}, s32[4]{0:T(128)S(1)}, /*index=5*/s32[4]{0:T(128)S(1)}, s32[4]{0:T(128)S(1)}, s32[4]{0:T(128)S(1)}) fusion(s32[8,4]{0,1:T(4,128)} %param.9), kind=kLoop, calls=%fused_computation.217 | loop fusion | flops 32 | bytes 256 | tf_op jit(solution)/shard_map/mul | solution.py:26
  10.8 1.1 %fusion.98 = (bf16[64,12,128]{2,1,0:T(8,128)(2,1)S(1)}, bf16[64,12,128]{2,1,0:T(8,128)(2,1)S(1)}) fusion(bf16[64,24,128]{2,1,0:T(8,128)(2,1)} %param.5), kind=kLoop, calls=%fused_computation.354 | loop fusion | bytes 786432 | tf_op jit(solution)/shard_map/slice | solution.py:23
  13.1 1.0 fusion.21
  15.1 0.5 copy.29
  16.2 0.5 copy.28
  18.4 0.5 copy.26
  21.7 0.5 copy.23
  23.3 1.0 bitcast_dynamic-update-slice_fusion.7
  24.3 1.0 bitcast_dynamic-update-slice_fusion.6
  25.3 1.0 bitcast_dynamic-update-slice_fusion.5
  26.3 1.0 bitcast_dynamic-update-slice_fusion.4
  27.3 1.0 bitcast_dynamic-update-slice_fusion.3
  28.3 1.0 bitcast_dynamic-update-slice_fusion.2
  29.3 2.6 %collective-permute-start.1 = (bf16[64,24,128]{2,1,0:T(8,128)(2,1)S(1)}, bf16[64,24,128]{2,1,0:T(8,128)(2,1)S(1)}, u32[]{:S(2)}, u32[]{:S(2)}) collective-permute-start(bf16[64,24,128]{2,1,0:T(8,128)(2,1)S(1)} %collective-permute-done), channel_id=1, source_target_pairs={{28,0},{0,4},{4,8},{8,12},{12,16},{16,20},{20,24},{24,28},{29,1},{... | collective-permute-start | bytes 1179656 | tf_op jit(solution)/shard_map/ppermute | solution.py:17
  31.9 1.0 bitcast_dynamic-update-slice_fusion.1
  32.9 4.7 %collective-permute-done.1 = bf16[64,24,128]{2,1,0:T(8,128)(2,1)S(1)} collective-permute-done((bf16[64,24,128]{2,1,0:T(8,128)(2,1)S(1)}, bf16[64,24,128]{2,1,0:T(8,128)(2,1)S(1)}, u32[]{:S(2)}, u32[]{:S(2)}) %collective-permute-start.1) | collective-permute-done | bytes 393248 | tf_op jit(solution)/shard_map/ppermute | solution.py:17
  37.7 1.1 bitcast_dynamic-update-slice_fusion
  39.1 6.7 %collective-permute-done.2 = bf16[64,24,128]{2,1,0:T(8,128)(2,1)S(1)} collective-permute-done((bf16[64,24,128]{2,1,0:T(8,128)(2,1)S(1)}, bf16[64,24,128]{2,1,0:T(8,128)(2,1)S(1)}, u32[]{:S(2)}, u32[]{:S(2)}) %collective-permute-start.2) | collective-permute-done | bytes 393248 | tf_op jit(solution)/shard_map/ppermute | solution.py:17
  45.9 5.5 %convolution_bitcast_fusion = f32[8,4,2,64,64]{4,3,1,2,0:T(8,128)S(1)} fusion(bf16[8,2,64,3072,1]{3,2,4,1,0:T(8,128)(2,1)} %bitcast.118, bf16[1,64,3072]{2,1,0:T(8,128)(2,1)S(1)} %stack.65, bf16[1,64,3072]{2,1,0:T(8,128)(2,1)S(1)} %stack.64, bf16[1,64,3072]{2,1,0:T(8,128)(2,1)S(1)} %stack.63, bf16[1,64,3072]{2,1,0:T(8,128)(2,1)S(1)} %stack.62), kind=kOutput, calls=%fused_computation.32 | convolution fusion | flops 1616904192 | bytes 8912896 | tf_op jit(solution)/shard_map/dot_general | solution.py:70
  51.5 1.5 %copy.30 = f32[8,4,2,64,64]{4,3,2,1,0:T(8,128)} copy(f32[8,4,2,64,64]{4,3,1,2,0:T(8,128)S(1)} %convolution_bitcast_fusion) | data formatting | bytes 2097152 | tf_op jit(solution)/shard_map/transpose | solution.py:73
  53.0 44.9 %reduce-scatter.2.cloned.1.call-done = f32[16,64,64]{2,1,0:T(8,128)} async-done(((f32[64,64,64]{2,1,0:T(8,128)}), f32[16,64,64]{2,1,0:T(8,128)}) %reduce-scatter.2.cloned.1.call-update) | async-done | bytes 262160 | tf_op jit(solution)/shard_map/reduce_scatter | solution.py:77
  97.9 1.9 %broadcast_multiply_fusion = f32[16,64,64]{2,1,0:T(8,128)} fusion(f32[16,64,64]{2,1,0:T(8,128)} %reduce-scatter.2.cloned.1.call-done), kind=kLoop, calls=%fused_computation.120 | loop fusion | flops 65536 | bytes 524288 | tf_op jit(solution)/shard_map/mul | solution.py:79
  (80 shorter events, 8.9 us)
Async XLA Ops:
  6.5 7.7 %copy-start = (s32[8,4]{0,1:T(4,128)S(1)}, s32[8,4]{0,1:T(4,128)}, u32[]{:S(2)}) copy-start(s32[8,4]{0,1:T(4,128)} %param.8) | copy-start | bytes 388
  6.5 91.3 %reduce-scatter.2.cloned.1.call-start = ((), (), s32[]{:S(2)}) async-start(), calls=%async_computation.1 | async-start | bytes 2621440 | tf_op jit(solution)/shard_map/reduce_scatter | solution.py:77
  6.5 22.8 %collective-permute-start = (bf16[64,24,128]{2,1,0:T(8,128)(2,1)}, bf16[64,24,128]{2,1,0:T(8,128)(2,1)S(1)}, u32[]{:S(2)}, u32[]{:S(2)}) collective-permute-start(bf16[64,24,128]{2,1,0:T(8,128)(2,1)} %param.6), channel_id=1, source_target_pairs={{28,0},{0,4},{4,8},{8,12},{12,16},{16,20},{20,24},{24,28},{29,1},{... | collective-permute-start | bytes 1179656 | tf_op jit(solution)/shard_map/ppermute | solution.py:17
  29.3 8.4 %collective-permute-start.1 = (bf16[64,24,128]{2,1,0:T(8,128)(2,1)S(1)}, bf16[64,24,128]{2,1,0:T(8,128)(2,1)S(1)}, u32[]{:S(2)}, u32[]{:S(2)}) collective-permute-start(bf16[64,24,128]{2,1,0:T(8,128)(2,1)S(1)} %collective-permute-done), channel_id=1, source_target_pairs={{28,0},{0,4},{4,8},{8,12},{12,16},{16,20},{20,24},{24,28},{29,1},{... | collective-permute-start | bytes 1179656 | tf_op jit(solution)/shard_map/ppermute | solution.py:17
  37.7 8.1 %collective-permute-start.2 = (bf16[64,24,128]{2,1,0:T(8,128)(2,1)S(1)}, bf16[64,24,128]{2,1,0:T(8,128)(2,1)S(1)}, u32[]{:S(2)}, u32[]{:S(2)}) collective-permute-start(bf16[64,24,128]{2,1,0:T(8,128)(2,1)S(1)} %collective-permute-done.1), channel_id=1, source_target_pairs={{28,0},{0,4},{4,8},{8,12},{12,16},{16,20},{20,24},{24,28},{29,1},{... | collective-permute-start | bytes 1179656 | tf_op jit(solution)/shard_map/ppermute | solution.py:17
Sparse Core Ops, SparseCore 0:
  53.1 44.6 reduce-scatter.1
where the time goes:
time: 107 us
  waiting for transfers between devices  56.3 us (53%)
  local copies, waits for them, and re-layouts  18.6 us (17%)
  between operations  13.9 us (13%)
  other arithmetic  9.1 us (9%)
  matrix products  5.55 us (5%)
  starting transfers between devices  3.12 us (3%)
    reduce_scatter x1, waiting for transfers between devices, local(): lax.psum_scatter(partial_value, 'space', scatter_dimension=0, tiled=True)  44.9 us
    ppermute x3, waiting for transfers between devices, from_behind(): return lax.ppermute(block, axis, route)  11.4 us
    unnamed x11, local copies, waits for them, and re-layouts  7.11 us
    dot_general x1, matrix products, local(): lax.dot_general(all_rows, rights, (((1,), (1,)), ((), ())), preferred_ele...  5.55 us
    another operation x8, local copies, waits for them, and re-layouts, turned_rows(): stacked = jnp.stack([re_rows, im_rows]).astype(jnp.bfloat16)  4.1 us
    ppermute x3, starting transfers between devices, from_behind(): return lax.ppermute(block, axis, route)  3.12 us
    another operation x8, other arithmetic  2.47 us
  transfers between devices with their start and end apart: 4, of which 3 were waited for; matrix products, arithmetic and copies ran while one was open for 23% of the time, Pallas kernels for 0%

commit v1 on v0

v1 whole, which is shorter than its diff:
```python
import functools
import math

import jax
import jax.numpy as jnp
from jax import lax
from jax.experimental import pallas as pl
from jax.experimental.pallas import tpu as pltpu
from jax.sharding import PartitionSpec as P


STRUCTS = 8
CYCLE = 4
LAT = 96
BOX = 16
LANES = 128
F32 = jnp.float32
BF16 = jnp.bfloat16
VMEM = pl.BlockSpec(memory_space=pltpu.VMEM)
SMEM = pl.BlockSpec(memory_space=pltpu.SMEM)
PARAMS = pltpu.CompilerParams(vmem_limit_bytes=16 << 20)


def routed(block, axis, source):
    size = lax.axis_size(axis)
    return lax.ppermute(block, axis, [(source(i) % size, i) for i in range(size)])


def build_rows(left, momenta, perm, phase, angle, cosine, sine, rows):
    modes = left.shape[0]
    structs = momenta.shape[1]
    sites = left.shape[1] // 24
    half = 12 * sites
    site = lax.axis_index("space") * sites + lax.broadcasted_iota(jnp.int32, (1, sites), 1)
    x = (site % BOX).astype(F32)
    y = (site // BOX % BOX).astype(F32)
    z = (site // (BOX * BOX)).astype(F32)
    for g in range(structs):
        dot = momenta[0, g].astype(F32) * x + momenta[1, g].astype(F32) * y + momenta[2, g].astype(F32) * z
        for a in range(4):
            angle[g * 4 + a : g * 4 + a + 1, :] = (LAT // 4 * phase[a, g]).astype(F32) - dot
    steps = angle[...]
    steps = steps - LAT * jnp.floor(steps * (1.0 / LAT))
    psi = steps * (2.0 * math.pi / LAT)
    cosine[...] = jnp.cos(psi)
    sine[...] = jnp.sin(psi)
    for a in range(4):
        for k in range(3):
            at = (a * 3 + k) * sites
            re = left[:, at : at + sites].astype(F32)
            im = left[:, half + at : half + at + sites].astype(F32)
            for g in range(structs):
                co = cosine[g * 4 + a : g * 4 + a + 1, :]
                si = sine[g * 4 + a : g * 4 + a + 1, :]
                to = pl.multiple_of((perm[a, g] * 3 + k) * sites, LANES)
                rows[g * modes : (g + 1) * modes, pl.ds(to, sites)] = (re * co + im * si).astype(BF16)
                to = pl.multiple_of(half + (perm[a, g] * 3 + k) * sites, LANES)
                rows[g * modes : (g + 1) * modes, pl.ds(to, sites)] = (im * co - re * si).astype(BF16)


def multiply(rows, right, both, total, sends, kept):
    modes, depth = right.shape
    half = depth // 2
    both[0:modes, :] = right[...]
    both[modes:, 0:half] = right[:, half:]
    both[modes:, half:] = -right[:, 0:half]
    total[...] = lax.dot_general(
        rows[...], both[...], (((1,), (1,)), ((), ())), preferred_element_type=F32
    ).reshape(total.shape)
    me = lax.axis_index("space")
    own = kept.shape[0]
    kept[...] = total[pl.ds(me * own, own)]
    for distance, send in enumerate(sends, 1):
        send[...] = total[pl.ds((me ^ distance) * own, own)].astype(BF16)


def first_kernel(n_send, left, right, momenta, perm, phase, rows, kept, *rest):
    sends, (angle, cosine, sine, both, total) = rest[:n_send], rest[n_send:]
    build_rows(left, momenta, perm, phase, angle, cosine, sine, rows)
    multiply(rows, right, both, total, sends, kept)


def next_kernel(n_send, rows, right, kept, *rest):
    sends, (both, total) = rest[:n_send], rest[n_send:]
    multiply(rows, right, both, total, sends, kept)


def join_kernel(groups, factor, *refs):
    out = refs[-1]
    each = (len(refs) - 1) // groups
    odd = lax.axis_index("mode") % 2
    places = (0, 1 + 2 * odd, 2, 3 - 2 * odd)
    modes = out.shape[1]
    for place, start in zip(places, range(0, groups * each, each)):
        for g in range(refs[start].shape[0]):
            value = refs[start][g]
            for part in refs[start + 1 : start + each]:
                value = value + part[g].astype(F32)
            value = value * factor
            for p in range(2):
                out[(g * CYCLE + place) * 2 + p] = value[:, p * modes : (p + 1) * modes]


def local(left_modes, right_modes, momenta, spin_perm, spin_phase):
    modes, comps, sites = left_modes.shape
    spaces = lax.axis_size("space")
    depth = comps * sites
    own = STRUCTS // spaces
    n_send = spaces - 1
    shape = jax.ShapeDtypeStruct
    outs = [shape((own, modes, 2 * modes), F32)] + [shape((own, modes, 2 * modes), BF16)] * n_send
    work = [pltpu.VMEM((2 * modes, depth), BF16), pltpu.VMEM((STRUCTS, modes, 2 * modes), F32)]

    ahead = routed(right_modes, "mode", lambda i: i - 1 if i % 2 == 0 else i - 3)
    far = routed(right_modes, "mode", lambda i: i - 3 if i % 2 == 0 else i - 1)
    swapped = routed(ahead, "mode", lambda i: i ^ 1)

    def exchange(group):
        kept, *sends = group
        return [kept] + [routed(s, "space", lambda i, d=d: i ^ d) for d, s in enumerate(sends, 1)]

    rows, *group = pl.pallas_call(
        functools.partial(first_kernel, n_send),
        out_shape=[shape((STRUCTS * modes, depth), BF16)] + outs,
        in_specs=[VMEM, VMEM, SMEM, SMEM, SMEM],
        out_specs=[VMEM] * (2 + n_send),
        scratch_shapes=[pltpu.VMEM((4 * STRUCTS, sites), F32)] * 3 + work,
        compiler_params=PARAMS,
        name="first",
    )(left_modes.reshape(modes, depth), right_modes.reshape(modes, depth), momenta.T, spin_perm.T, spin_phase.T)
    received = exchange(group)
    for block in (ahead, swapped, far):
        group = pl.pallas_call(
            functools.partial(next_kernel, n_send),
            out_shape=outs,
            in_specs=[VMEM, VMEM],
            out_specs=[VMEM] * (1 + n_send),
            scratch_shapes=work,
            compiler_params=PARAMS,
            name="next",
        )(rows, block.reshape(modes, depth))
        received += exchange(group)
    return pl.pallas_call(
        functools.partial(join_kernel, CYCLE, 1.0 / math.sqrt(depth * spaces)),
        out_shape=shape((own * CYCLE * 2, modes, modes), F32),
        in_specs=[VMEM] * len(received),
        out_specs=VMEM,
        compiler_params=PARAMS,
        name="join",
    )(*received)


def turned_rows(mode_rows, momenta, spin_perm, spin_phase, coords, struct_id):
    mode_count = mode_rows.shape[0]
    site_count = mode_rows.shape[2]
    real_part = mode_rows[:, :12, :].astype(F32).reshape(mode_count, 4, 3, site_count)
    imag_part = mode_rows[:, 12:, :].astype(F32).reshape(mode_count, 4, 3, site_count)
    momentum_dot = jnp.sum(momenta[struct_id][:, None] * coords, axis=0)
    quarter = jnp.mod(LAT // 4 * spin_phase[struct_id][:, None] - momentum_dot[None, :], LAT)
    phase_angle = quarter.astype(F32) * (2.0 * math.pi / LAT)
    cosine = jnp.cos(phase_angle)[None, :, None, :]
    sine_val = jnp.sin(phase_angle)[None, :, None, :]
    turn_re = real_part * cosine + imag_part * sine_val
    turn_im = imag_part * cosine - real_part * sine_val
    chooser = (spin_perm[struct_id][:, None] == jnp.arange(4, dtype=jnp.int32)[None, :]).astype(F32)
    moved_re = chooser[0][None, :, None, None] * turn_re[:, 0:1]
    moved_im = chooser[0][None, :, None, None] * turn_im[:, 0:1]
    for a in range(1, 4):
        moved_re = moved_re + chooser[a][None, :, None, None] * turn_re[:, a : a + 1]
        moved_im = moved_im + chooser[a][None, :, None, None] * turn_im[:, a : a + 1]
    re_rows = jnp.concatenate([moved_re, moved_im], axis=1).reshape(mode_count, 24, site_count)
    im_rows = jnp.concatenate([-moved_im, moved_re], axis=1).reshape(mode_count, 24, site_count)
    return jnp.stack([re_rows, im_rows]).astype(BF16).reshape(2 * mode_count, 24 * site_count)


def plain_local(left_modes, right_modes, momenta, spin_perm, spin_phase):
    mode_count, comp_count, site_count = left_modes.shape
    space_count = lax.axis_size("space")
    site_index = lax.axis_index("space") * site_count + lax.iota(jnp.int32, site_count)
    coords = jnp.stack([site_index % BOX, site_index // BOX % BOX, site_index // (BOX * BOX)])
    blocks = [right_modes]
    for _ in range(1, CYCLE):
        blocks.append(routed(blocks[-1], "mode", lambda i: i - 1))
    rights = jnp.stack(blocks).reshape(CYCLE * mode_count, comp_count * site_count)
    all_rows = jnp.concatenate(
        [turned_rows(left_modes, momenta, spin_perm, spin_phase, coords, g) for g in range(STRUCTS)], axis=0
    )
    product = lax.dot_general(all_rows, rights, (((1,), (1,)), ((), ())), preferred_element_type=F32)
    partial_value = product.reshape(STRUCTS, 2, mode_count, CYCLE, mode_count).transpose(0, 3, 1, 2, 4)
    partial_value = partial_value.reshape(STRUCTS * CYCLE * 2, mode_count, mode_count)
    owned = lax.psum_scatter(partial_value, "space", scatter_dimension=0, tiled=True)
    return owned * (1.0 / math.sqrt(24 * site_count * space_count))


def solution(mesh):
    spaces, n_mode = mesh.shape["space"], mesh.shape["mode"]
    fits = spaces & (spaces - 1) == 0 and STRUCTS % spaces == 0 and n_mode % 2 == 0 and n_mode >= CYCLE

    def either(left_modes, *rest):
        body = local if fits and left_modes.shape[2] % LANES == 0 else plain_local
        return body(left_modes, *rest)

    placed = (P("mode", None, "space"), P("mode", None, "space"), P(), P(), P())
    return jax.shard_map(
        either, mesh=mesh, in_specs=placed, out_specs=P("space", "mode", None), check_vma=False
    )
```

time: 107 us -> 48.6 us (0.45)
  waiting for transfers between devices: 56.3 us -> 15.1 us
  starting transfers between devices: 3.12 us -> 22.3 us
  local copies, waits for them, and re-layouts: 18.6 us -> 4.31 us
  between operations: 13.9 us -> 0.11 us
  other arithmetic: 9.1 us -> 0 us
  Pallas kernels: 0 us -> 6.54 us
  matrix products: 5.55 us -> 0 us
    reduce_scatter x1 -> x0, waiting for transfers between devices: 44.9 us -> none  [local(): lax.psum_scatter(partial_value, 'space', scatter_dimension=0, tiled=True)]
    ppermute x3 -> x15, starting transfers between devices: 3.12 us -> 22.3 us  [routed(): lax.ppermute(block, axis, [(source(i) % size, i) for i in range(size)])]
    pallas_call x0 -> x5, Pallas kernels: none -> 6.54 us  [the longest x3 2.98 us: local(): pl.pallas_call(functools.partial(next_kernel, n_send), out_shape=outs, in...]
    another operation x12 -> x0, local copies, waits for them, and re-layouts: 5.77 us -> none  [the longest x8 4.1 us: turned_rows(): stacked = jnp.stack([re_rows, im_rows]).astype(jnp.bfloat16)]
    dot_general x1 -> x0, matrix products: 5.55 us -> none  [local(): lax.dot_general(all_rows, rights, (((1,), (1,)), ((), ())), preferred_ele...]
    ppermute x3 -> x15, waiting for transfers between devices: 11.4 us -> 15.1 us  [routed(): lax.ppermute(block, axis, [(source(i) % size, i) for i in range(size)])]
    mul x2 -> x0, other arithmetic: 3.17 us -> none  [the longest x1 1.89 us: local(): return owned * factor]
    another operation x16 -> x0, other arithmetic: 3.08 us -> none
  transfers between devices with their start and end apart: 4 -> 15, of which waited for: 3 -> 4; matrix products, arithmetic and copies ran while one was open for 23% -> 5% of each run, Pallas kernels for 0% -> 12%
where the time goes in v1:
time: 48.6 us; the launch traced here: 48.4 us
  starting transfers between devices  22.3 us (46%)
  waiting for transfers between devices  15.1 us (31%)
  Pallas kernels  6.54 us (13%)
  local copies, waits for them, and re-layouts  4.31 us (9%)
    ppermute x15, starting transfers between devices, routed(): lax.ppermute(block, axis, [(source(i) % size, i) for i in range(size)])  22.3 us
    ppermute x15, waiting for transfers between devices, routed(): lax.ppermute(block, axis, [(source(i) % size, i) for i in range(size)])  15.1 us
    unnamed x11, local copies, waits for them, and re-layouts  4.31 us
    pallas_call x3, Pallas kernels, local(): pl.pallas_call(functools.partial(next_kernel, n_send), out_shape=outs, in...  2.98 us
    pallas_call x1, Pallas kernels, local(): pl.pallas_call(functools.partial(first_kernel, n_send), out_shape=[shape(...  2.62 us
  transfers between devices with their start and end apart: 15, of which 4 were waited for; matrix products, arithmetic and copies ran while one was open for 5% of the time, Pallas kernels for 12%

profile of v1, /device:TPU:0, one launch (start us, length us, event | category | flops | bytes accessed | tf_op | source)
XLA Modules:
  0.0 48.4 jit_solution(14577531414239742187)
XLA Ops:
  0.0 2.4 %collective-permute-start.3 = (bf16[64,24,128]{2,1,0:T(8,128)(2,1)}, bf16[64,24,128]{2,1,0:T(8,128)(2,1)S(1)}, u32[]{:S(2)}, u32[]{:S(2)}) collective-permute-start(bf16[64,24,128]{2,1,0:T(8,128)(2,1)} %param.6), channel_id=1, source_target_pairs={{28,0},{24,4},{4,8},{0,12},{12,16},{8,20},{20,24},{16,28},{29,1},{... | collective-permute-start | bytes 1179656 | tf_op jit(solution)/shard_map/ppermute | solution.py:26
  2.4 0.7 %collective-permute-start.11 = (bf16[64,24,128]{2,1,0:T(8,128)(2,1)}, bf16[64,24,128]{2,1,0:T(8,128)(2,1)S(1)}, u32[]{:S(2)}, u32[]{:S(2)}) collective-permute-start(bf16[64,24,128]{2,1,0:T(8,128)(2,1)} %param.6), channel_id=1, source_target_pairs={{20,0},{0,4},{28,8},{8,12},{4,16},{16,20},{12,24},{24,28},{21,1},{... | collective-permute-start | bytes 1179656 | tf_op jit(solution)/shard_map/ppermute | solution.py:26
  3.1 9.4 %collective-permute-done.3 = bf16[64,24,128]{2,1,0:T(8,128)(2,1)S(1)} collective-permute-done((bf16[64,24,128]{2,1,0:T(8,128)(2,1)}, bf16[64,24,128]{2,1,0:T(8,128)(2,1)S(1)}, u32[]{:S(2)}, u32[]{:S(2)}) %collective-permute-start.3) | collective-permute-done | bytes 393248 | tf_op jit(solution)/shard_map/ppermute | solution.py:26
  12.5 0.7 %collective-permute-start.7 = (bf16[64,24,128]{2,1,0:T(8,128)(2,1)S(1)}, bf16[64,24,128]{2,1,0:T(8,128)(2,1)S(1)}, u32[]{:S(2)}, u32[]{:S(2)}) collective-permute-start(bf16[64,24,128]{2,1,0:T(8,128)(2,1)S(1)} %collective-permute-done.3), channel_id=1, source_target_pairs={{4,0},{0,4},{12,8},{8,12},{20,16},{16,20},{28,24},{24,28},{5,1},{1... | collective-permute-start | bytes 1179656 | tf_op jit(solution)/shard_map/ppermute | solution.py:26
  13.2 1.1 %copy.20 = bf16[8,8,24,128]{3,1,2,0:T(8,128)(2,1)S(1)} copy(bf16[8,8,24,128]{3,2,1,0:T(8,128)(2,1)} %bitcast.31) | data formatting | bytes 786432
  14.2 1.1 %copy.19 = bf16[8,8,24,128]{3,1,2,0:T(8,128)(2,1)S(1)} copy(bf16[8,8,24,128]{3,2,1,0:T(8,128)(2,1)} %bitcast.32) | data formatting | bytes 786432
  15.3 0.7 %copy-done = s32[8,3]{0,1:T(4,128)S(1)} copy-done((s32[8,3]{0,1:T(4,128)S(1)}, s32[8,3]{0,1:T(4,128)}, u32[]{:S(2)}) %copy-start) | copy-done | bytes 120
  16.0 0.7 %copy-done.1 = s32[8,4]{0,1:T(4,128)S(1)} copy-done((s32[8,4]{0,1:T(4,128)S(1)}, s32[8,4]{0,1:T(4,128)}, u32[]{:S(2)}) %copy-start.1) | copy-done | bytes 152
  16.7 0.7 %copy-done.2 = s32[8,4]{0,1:T(4,128)S(1)} copy-done((s32[8,4]{0,1:T(4,128)S(1)}, s32[8,4]{0,1:T(4,128)}, u32[]{:S(2)}) %copy-start.2) | copy-done | bytes 152
  17.3 2.6 %first.1 = (bf16[512,3072]{1,0:T(8,128)(2,1)S(1)}, f32[2,64,128]{2,1,0:T(8,128)S(1)}, bf16[2,64,128]{2,1,0:T(8,128)(2,1)S(1)}, bf16[2,64,128]{2,1,0:T(8,128)(2,1)S(1)}, bf16[2,64,128]{2,1,0:T(8,128)(2,1)S(1)}) custom-call(bf16[64,3072]{1,0:T(8,128)(2,1)S(1)} %bitcast.23, bf16[64,3072]{1,0:T(8,128)(2,1)S(1)} %bitcast.24, s32[3,8]{1,0:T(4,128)S(1)} %bitcast.28, ...), custom_call_target="tpu_custom_call" | custom-call | tf_op jit(solution)/shard_map/first/pallas_call | solution.py:122
  20.0 2.5 %collective-permute-start = (bf16[2,64,128]{2,1,0:T(8,128)(2,1)S(1)}, bf16[2,64,128]{2,1,0:T(8,128)(2,1)S(1)}, u32[]{:S(2)}, u32[]{:S(2)}) collective-permute-start(bf16[2,64,128]{2,1,0:T(8,128)(2,1)S(1)} %get-tuple-element.23), channel_id=1, source_target_pairs={{1,0},{0,1},{3,2},{2,3},{5,4},{4,5},{7,6},{6,7},{9,8},{8,9},{11,10... | collective-permute-start | bytes 98312 | tf_op jit(solution)/shard_map/ppermute | solution.py:26
  22.5 2.6 %collective-permute-start.1 = (bf16[2,64,128]{2,1,0:T(8,128)(2,1)S(1)}, bf16[2,64,128]{2,1,0:T(8,128)(2,1)S(1)}, u32[]{:S(2)}, u32[]{:S(2)}) collective-permute-start(bf16[2,64,128]{2,1,0:T(8,128)(2,1)S(1)} %get-tuple-element.24), channel_id=1, source_target_pairs={{2,0},{3,1},{0,2},{1,3},{6,4},{7,5},{4,6},{5,7},{10,8},{11,9},{8,1... | collective-permute-start | bytes 98312 | tf_op jit(solution)/shard_map/ppermute | solution.py:26
  25.2 1.0 %next.3 = (f32[2,64,128]{2,1,0:T(8,128)S(1)}, bf16[2,64,128]{2,1,0:T(8,128)(2,1)S(1)}, bf16[2,64,128]{2,1,0:T(8,128)(2,1)S(1)}, bf16[2,64,128]{2,1,0:T(8,128)(2,1)S(1)}) custom-call(bf16[512,3072]{1,0:T(8,128)(2,1)S(1)} %get-tuple-element.26.rows, bf16[64,3072]{1,0:T(8,128)(2,1)S(1)} %bitcast.27), custom_call_target="tpu_custom_call" | custom-call | tf_op jit(solution)/shard_map/next/pallas_call | solution.py:133
  26.2 1.0 %collective-permute-start.4 = (bf16[2,64,128]{2,1,0:T(8,128)(2,1)S(1)}, bf16[2,64,128]{2,1,0:T(8,128)(2,1)S(1)}, u32[]{:S(2)}, u32[]{:S(2)}) collective-permute-start(bf16[2,64,128]{2,1,0:T(8,128)(2,1)S(1)} %get-tuple-element.28), channel_id=1, source_target_pairs={{1,0},{0,1},{3,2},{2,3},{5,4},{4,5},{7,6},{6,7},{9,8},{8,9},{11,10... | collective-permute-start | bytes 98312 | tf_op jit(solution)/shard_map/ppermute | solution.py:26
  27.2 1.0 %next.5 = (f32[2,64,128]{2,1,0:T(8,128)S(1)}, bf16[2,64,128]{2,1,0:T(8,128)(2,1)S(1)}, bf16[2,64,128]{2,1,0:T(8,128)(2,1)S(1)}, bf16[2,64,128]{2,1,0:T(8,128)(2,1)S(1)}) custom-call(bf16[512,3072]{1,0:T(8,128)(2,1)S(1)} %get-tuple-element.26.rows, bf16[64,3072]{1,0:T(8,128)(2,1)S(1)} %bitcast.26), custom_call_target="tpu_custom_call" | custom-call | tf_op jit(solution)/shard_map/next/pallas_call | solution.py:133
  28.2 3.6 %collective-permute-start.5 = (bf16[2,64,128]{2,1,0:T(8,128)(2,1)S(1)}, bf16[2,64,128]{2,1,0:T(8,128)(2,1)S(1)}, u32[]{:S(2)}, u32[]{:S(2)}) collective-permute-start(bf16[2,64,128]{2,1,0:T(8,128)(2,1)S(1)} %get-tuple-element.29), channel_id=1, source_target_pairs={{2,0},{3,1},{0,2},{1,3},{6,4},{7,5},{4,6},{5,7},{10,8},{11,9},{8,1... | collective-permute-start | bytes 98312 | tf_op jit(solution)/shard_map/ppermute | solution.py:26
  31.8 0.6 %collective-permute-start.12 = (bf16[2,64,128]{2,1,0:T(8,128)(2,1)S(1)}, bf16[2,64,128]{2,1,0:T(8,128)(2,1)S(1)}, u32[]{:S(2)}, u32[]{:S(2)}) collective-permute-start(bf16[2,64,128]{2,1,0:T(8,128)(2,1)S(1)} %get-tuple-element.36), channel_id=1, source_target_pairs={{1,0},{0,1},{3,2},{2,3},{5,4},{4,5},{7,6},{6,7},{9,8},{8,9},{11,10... | collective-permute-start | bytes 98312 | tf_op jit(solution)/shard_map/ppermute | solution.py:26
  32.5 1.0 %next.4 = (f32[2,64,128]{2,1,0:T(8,128)S(1)}, bf16[2,64,128]{2,1,0:T(8,128)(2,1)S(1)}, bf16[2,64,128]{2,1,0:T(8,128)(2,1)S(1)}, bf16[2,64,128]{2,1,0:T(8,128)(2,1)S(1)}) custom-call(bf16[512,3072]{1,0:T(8,128)(2,1)S(1)} %get-tuple-element.26.rows, bf16[64,3072]{1,0:T(8,128)(2,1)S(1)} %bitcast.25), custom_call_target="tpu_custom_call" | custom-call | tf_op jit(solution)/shard_map/next/pallas_call | solution.py:133
  33.5 3.8 %collective-permute-start.13 = (bf16[2,64,128]{2,1,0:T(8,128)(2,1)S(1)}, bf16[2,64,128]{2,1,0:T(8,128)(2,1)S(1)}, u32[]{:S(2)}, u32[]{:S(2)}) collective-permute-start(bf16[2,64,128]{2,1,0:T(8,128)(2,1)S(1)} %get-tuple-element.37), channel_id=1, source_target_pairs={{2,0},{3,1},{0,2},{1,3},{6,4},{7,5},{4,6},{5,7},{10,8},{11,9},{8,1... | collective-permute-start | bytes 98312 | tf_op jit(solution)/shard_map/ppermute | solution.py:26
  38.0 3.7 %collective-permute-start.9 = (bf16[2,64,128]{2,1,0:T(8,128)(2,1)S(1)}, bf16[2,64,128]{2,1,0:T(8,128)(2,1)S(1)}, u32[]{:S(2)}, u32[]{:S(2)}) collective-permute-start(bf16[2,64,128]{2,1,0:T(8,128)(2,1)S(1)} %get-tuple-element.33), channel_id=1, source_target_pairs={{2,0},{3,1},{0,2},{1,3},{6,4},{7,5},{4,6},{5,7},{10,8},{11,9},{8,1... | collective-permute-start | bytes 98312 | tf_op jit(solution)/shard_map/ppermute | solution.py:26
  41.8 1.2 %collective-permute-done.14.refs_15_ = bf16[2,64,128]{2,1,0:T(8,128)(2,1)S(1)} collective-permute-done((bf16[2,64,128]{2,1,0:T(8,128)(2,1)S(1)}, bf16[2,64,128]{2,1,0:T(8,128)(2,1)S(1)}, u32[]{:S(2)}, u32[]{:S(2)}) %collective-permute-start.14) | collective-permute-done | bytes 32800 | tf_op jit(solution)/shard_map/ppermute | solution.py:26
  43.0 1.3 %collective-permute-done.9.refs_10_ = bf16[2,64,128]{2,1,0:T(8,128)(2,1)S(1)} collective-permute-done((bf16[2,64,128]{2,1,0:T(8,128)(2,1)S(1)}, bf16[2,64,128]{2,1,0:T(8,128)(2,1)S(1)}, u32[]{:S(2)}, u32[]{:S(2)}) %collective-permute-start.9) | collective-permute-done | bytes 32800 | tf_op jit(solution)/shard_map/ppermute | solution.py:26
  44.3 3.1 %collective-permute-done.10.refs_11_ = bf16[2,64,128]{2,1,0:T(8,128)(2,1)S(1)} collective-permute-done((bf16[2,64,128]{2,1,0:T(8,128)(2,1)S(1)}, bf16[2,64,128]{2,1,0:T(8,128)(2,1)S(1)}, u32[]{:S(2)}, u32[]{:S(2)}) %collective-permute-start.10) | collective-permute-done | bytes 32800 | tf_op jit(solution)/shard_map/ppermute | solution.py:26
  47.4 0.9 %join.1 = f32[16,64,64]{2,1,0:T(8,128)} custom-call(f32[2,64,128]{2,1,0:T(8,128)S(1)} %get-tuple-element.22.refs_0_, bf16[2,64,128]{2,1,0:T(8,128)(2,1)S(1)} %collective-permute-done.refs_1_, bf16[2,64,128]{2,1,0:T(8,128)(2,1)S(1)} %collective-permute-done.1.refs_2_, bf16[2,64,128]{2,1,0:T(8,128)(2,1)S(1)} %collective-permute-done.2.refs_3_, ...), custom_call_target="tpu_custom_call" | custom-call | tf_op jit(solution)/shard_map/join/pallas_call | solution.py:143
  (22 shorter events, 0.9 us)
Async XLA Ops:
  0.0 12.5 %collective-permute-start.3 = (bf16[64,24,128]{2,1,0:T(8,128)(2,1)}, bf16[64,24,128]{2,1,0:T(8,128)(2,1)S(1)}, u32[]{:S(2)}, u32[]{:S(2)}) collective-permute-start(bf16[64,24,128]{2,1,0:T(8,128)(2,1)} %param.6), channel_id=1, source_target_pairs={{28,0},{24,4},{4,8},{0,12},{12,16},{8,20},{20,24},{16,28},{29,1},{... | collective-permute-start | bytes 1179656 | tf_op jit(solution)/shard_map/ppermute | solution.py:26
  2.4 23.8 %collective-permute-start.11 = (bf16[64,24,128]{2,1,0:T(8,128)(2,1)}, bf16[64,24,128]{2,1,0:T(8,128)(2,1)S(1)}, u32[]{:S(2)}, u32[]{:S(2)}) collective-permute-start(bf16[64,24,128]{2,1,0:T(8,128)(2,1)} %param.6), channel_id=1, source_target_pairs={{20,0},{0,4},{28,8},{8,12},{4,16},{16,20},{12,24},{24,28},{21,1},{... | collective-permute-start | bytes 1179656 | tf_op jit(solution)/shard_map/ppermute | solution.py:26
  12.5 19.3 %collective-permute-start.7 = (bf16[64,24,128]{2,1,0:T(8,128)(2,1)S(1)}, bf16[64,24,128]{2,1,0:T(8,128)(2,1)S(1)}, u32[]{:S(2)}, u32[]{:S(2)}) collective-permute-start(bf16[64,24,128]{2,1,0:T(8,128)(2,1)S(1)} %collective-permute-done.3), channel_id=1, source_target_pairs={{4,0},{0,4},{12,8},{8,12},{20,16},{16,20},{28,24},{24,28},{5,1},{1... | collective-permute-start | bytes 1179656 | tf_op jit(solution)/shard_map/ppermute | solution.py:26
  15.3 0.7 %copy-start = (s32[8,3]{0,1:T(4,128)S(1)}, s32[8,3]{0,1:T(4,128)}, u32[]{:S(2)}) copy-start(s32[8,3]{0,1:T(4,128)} %param.7) | copy-start | bytes 292
  16.0 0.7 %copy-start.1 = (s32[8,4]{0,1:T(4,128)S(1)}, s32[8,4]{0,1:T(4,128)}, u32[]{:S(2)}) copy-start(s32[8,4]{0,1:T(4,128)} %param.8) | copy-start | bytes 388
  16.7 0.7 %copy-start.2 = (s32[8,4]{0,1:T(4,128)S(1)}, s32[8,4]{0,1:T(4,128)}, u32[]{:S(2)}) copy-start(s32[8,4]{0,1:T(4,128)} %param.9) | copy-start | bytes 388
  20.0 8.2 %collective-permute-start = (bf16[2,64,128]{2,1,0:T(8,128)(2,1)S(1)}, bf16[2,64,128]{2,1,0:T(8,128)(2,1)S(1)}, u32[]{:S(2)}, u32[]{:S(2)}) collective-permute-start(bf16[2,64,128]{2,1,0:T(8,128)(2,1)S(1)} %get-tuple-element.23), channel_id=1, source_target_pairs={{1,0},{0,1},{3,2},{2,3},{5,4},{4,5},{7,6},{6,7},{9,8},{8,9},{11,10... | collective-permute-start | bytes 98312 | tf_op jit(solution)/shard_map/ppermute | solution.py:26
  22.5 9.3 %collective-permute-start.1 = (bf16[2,64,128]{2,1,0:T(8,128)(2,1)S(1)}, bf16[2,64,128]{2,1,0:T(8,128)(2,1)S(1)}, u32[]{:S(2)}, u32[]{:S(2)}) collective-permute-start(bf16[2,64,128]{2,1,0:T(8,128)(2,1)S(1)} %get-tuple-element.24), channel_id=1, source_target_pairs={{2,0},{3,1},{0,2},{1,3},{6,4},{7,5},{4,6},{5,7},{10,8},{11,9},{8,1... | collective-permute-start | bytes 98312 | tf_op jit(solution)/shard_map/ppermute | solution.py:26
  25.1 8.4 %collective-permute-start.2 = (bf16[2,64,128]{2,1,0:T(8,128)(2,1)S(1)}, bf16[2,64,128]{2,1,0:T(8,128)(2,1)S(1)}, u32[]{:S(2)}, u32[]{:S(2)}) collective-permute-start(bf16[2,64,128]{2,1,0:T(8,128)(2,1)S(1)} %get-tuple-element.25), channel_id=1, source_target_pairs={{3,0},{2,1},{1,2},{0,3},{7,4},{6,5},{5,6},{4,7},{11,8},{10,9},{9,1... | collective-permute-start | bytes 98312 | tf_op jit(solution)/shard_map/ppermute | solution.py:26
  26.2 11.1 %collective-permute-start.4 = (bf16[2,64,128]{2,1,0:T(8,128)(2,1)S(1)}, bf16[2,64,128]{2,1,0:T(8,128)(2,1)S(1)}, u32[]{:S(2)}, u32[]{:S(2)}) collective-permute-start(bf16[2,64,128]{2,1,0:T(8,128)(2,1)S(1)} %get-tuple-element.28), channel_id=1, source_target_pairs={{1,0},{0,1},{3,2},{2,3},{5,4},{4,5},{7,6},{6,7},{9,8},{8,9},{11,10... | collective-permute-start | bytes 98312 | tf_op jit(solution)/shard_map/ppermute | solution.py:26
  28.2 9.2 %collective-permute-start.5 = (bf16[2,64,128]{2,1,0:T(8,128)(2,1)S(1)}, bf16[2,64,128]{2,1,0:T(8,128)(2,1)S(1)}, u32[]{:S(2)}, u32[]{:S(2)}) collective-permute-start(bf16[2,64,128]{2,1,0:T(8,128)(2,1)S(1)} %get-tuple-element.29), channel_id=1, source_target_pairs={{2,0},{3,1},{0,2},{1,3},{6,4},{7,5},{4,6},{5,7},{10,8},{11,9},{8,1... | collective-permute-start | bytes 98312 | tf_op jit(solution)/shard_map/ppermute | solution.py:26
  31.8 6.2 %collective-permute-start.6 = (bf16[2,64,128]{2,1,0:T(8,128)(2,1)S(1)}, bf16[2,64,128]{2,1,0:T(8,128)(2,1)S(1)}, u32[]{:S(2)}, u32[]{:S(2)}) collective-permute-start(bf16[2,64,128]{2,1,0:T(8,128)(2,1)S(1)} %get-tuple-element.30), channel_id=1, source_target_pairs={{3,0},{2,1},{1,2},{0,3},{7,4},{6,5},{5,6},{4,7},{11,8},{10,9},{9,1... | collective-permute-start | bytes 98312 | tf_op jit(solution)/shard_map/ppermute | solution.py:26
  31.8 9.9 %collective-permute-start.12 = (bf16[2,64,128]{2,1,0:T(8,128)(2,1)S(1)}, bf16[2,64,128]{2,1,0:T(8,128)(2,1)S(1)}, u32[]{:S(2)}, u32[]{:S(2)}) collective-permute-start(bf16[2,64,128]{2,1,0:T(8,128)(2,1)S(1)} %get-tuple-element.36), channel_id=1, source_target_pairs={{1,0},{0,1},{3,2},{2,3},{5,4},{4,5},{7,6},{6,7},{9,8},{8,9},{11,10... | collective-permute-start | bytes 98312 | tf_op jit(solution)/shard_map/ppermute | solution.py:26
  33.5 8.3 %collective-permute-start.13 = (bf16[2,64,128]{2,1,0:T(8,128)(2,1)S(1)}, bf16[2,64,128]{2,1,0:T(8,128)(2,1)S(1)}, u32[]{:S(2)}, u32[]{:S(2)}) collective-permute-start(bf16[2,64,128]{2,1,0:T(8,128)(2,1)S(1)} %get-tuple-element.37), channel_id=1, source_target_pairs={{2,0},{3,1},{0,2},{1,3},{6,4},{7,5},{4,6},{5,7},{10,8},{11,9},{8,1... | collective-permute-start | bytes 98312 | tf_op jit(solution)/shard_map/ppermute | solution.py:26
  37.3 5.7 %collective-permute-start.14 = (bf16[2,64,128]{2,1,0:T(8,128)(2,1)S(1)}, bf16[2,64,128]{2,1,0:T(8,128)(2,1)S(1)}, u32[]{:S(2)}, u32[]{:S(2)}) collective-permute-start(bf16[2,64,128]{2,1,0:T(8,128)(2,1)S(1)} %get-tuple-element.38), channel_id=1, source_target_pairs={{3,0},{2,1},{1,2},{0,3},{7,4},{6,5},{5,6},{4,7},{11,8},{10,9},{9,1... | collective-permute-start | bytes 98312 | tf_op jit(solution)/shard_map/ppermute | solution.py:26
  37.4 5.6 %collective-permute-start.8 = (bf16[2,64,128]{2,1,0:T(8,128)(2,1)S(1)}, bf16[2,64,128]{2,1,0:T(8,128)(2,1)S(1)}, u32[]{:S(2)}, u32[]{:S(2)}) collective-permute-start(bf16[2,64,128]{2,1,0:T(8,128)(2,1)S(1)} %get-tuple-element.32), channel_id=1, source_target_pairs={{1,0},{0,1},{3,2},{2,3},{5,4},{4,5},{7,6},{6,7},{9,8},{8,9},{11,10... | collective-permute-start | bytes 98312 | tf_op jit(solution)/shard_map/ppermute | solution.py:26
  38.0 6.3 %collective-permute-start.9 = (bf16[2,64,128]{2,1,0:T(8,128)(2,1)S(1)}, bf16[2,64,128]{2,1,0:T(8,128)(2,1)S(1)}, u32[]{:S(2)}, u32[]{:S(2)}) collective-permute-start(bf16[2,64,128]{2,1,0:T(8,128)(2,1)S(1)} %get-tuple-element.33), channel_id=1, source_target_pairs={{2,0},{3,1},{0,2},{1,3},{6,4},{7,5},{4,6},{5,7},{10,8},{11,9},{8,1... | collective-permute-start | bytes 98312 | tf_op jit(solution)/shard_map/ppermute | solution.py:26
  41.7 5.7 %collective-permute-start.10 = (bf16[2,64,128]{2,1,0:T(8,128)(2,1)S(1)}, bf16[2,64,128]{2,1,0:T(8,128)(2,1)S(1)}, u32[]{:S(2)}, u32[]{:S(2)}) collective-permute-start(bf16[2,64,128]{2,1,0:T(8,128)(2,1)S(1)} %get-tuple-element.34), channel_id=1, source_target_pairs={{3,0},{2,1},{1,2},{0,3},{7,4},{6,5},{5,6},{4,7},{11,8},{10,9},{9,1... | collective-permute-start | bytes 98312 | tf_op jit(solution)/shard_map/ppermute | solution.py:26

commit v2 on v1

--- a/solution.py
+++ b/solution.py
@@ -58,7 +58,7 @@
                 rows[g * modes : (g + 1) * modes, pl.ds(to, sites)] = (im * co - re * si).astype(BF16)
 
 
-def multiply(rows, right, both, total, sends, kept):
+def multiply(rows, right, both, total, sends, kept, slot=0):
     modes, depth = right.shape
     half = depth // 2
     both[0:modes, :] = right[...]
@@ -68,10 +68,10 @@
         rows[...], both[...], (((1,), (1,)), ((), ())), preferred_element_type=F32
     ).reshape(total.shape)
     me = lax.axis_index("space")
-    own = kept.shape[0]
-    kept[...] = total[pl.ds(me * own, own)]
+    own = kept.shape[1]
+    kept[slot] = total[pl.ds(me * own, own)]
     for distance, send in enumerate(sends, 1):
-        send[...] = total[pl.ds((me ^ distance) * own, own)].astype(BF16)
+        send[slot] = total[pl.ds((me ^ distance) * own, own)].astype(BF16)
 
 
 def first_kernel(n_send, left, right, momenta, perm, phase, rows, kept, *rest):
@@ -85,20 +85,28 @@
     multiply(rows, right, both, total, sends, kept)
 
 
-def join_kernel(groups, factor, *refs):
+def add_kernel(n_send, rows, right, *rest):
+    before, after, (both, total) = rest[: 1 + n_send], rest[1 + n_send : 2 + 2 * n_send], rest[2 + 2 * n_send :]
+    for old, new in zip(before, after):
+        new[0:1] = old[...]
+    multiply(rows, right, both, total, after[1:], after[0], 1)
+
+
+def join_kernel(spaces, factor, *refs):
     out = refs[-1]
-    each = (len(refs) - 1) // groups
     odd = lax.axis_index("mode") % 2
-    places = (0, 1 + 2 * odd, 2, 3 - 2 * odd)
+    places = iter((0, 1 + 2 * odd, 2, 3 - 2 * odd))
     modes = out.shape[1]
-    for place, start in zip(places, range(0, groups * each, each)):
-        for g in range(refs[start].shape[0]):
-            value = refs[start][g]
-            for part in refs[start + 1 : start + each]:
-                value = value + part[g].astype(F32)
-            value = value * factor
-            for p in range(2):
-                out[(g * CYCLE + place) * 2 + p] = value[:, p * modes : (p + 1) * modes]
+    for start in range(0, len(refs) - 1, spaces):
+        for slot in range(refs[start].shape[0]):
+            place = next(places)
+            for g in range(refs[start].shape[1]):
+                value = refs[start][slot, g]
+                for part in refs[start + 1 : start + spaces]:
+                    value = value + part[slot, g].astype(F32)
+                value = value * factor
+                for p in range(2):
+                    out[(g * CYCLE + place) * 2 + p] = value[:, p * modes : (p + 1) * modes]
 
 
 def local(left_modes, right_modes, momenta, spin_perm, spin_phase):
@@ -108,7 +116,11 @@
     own = STRUCTS // spaces
     n_send = spaces - 1
     shape = jax.ShapeDtypeStruct
-    outs = [shape((own, modes, 2 * modes), F32)] + [shape((own, modes, 2 * modes), BF16)] * n_send
+
+    def outs(slots):
+        size = (slots, own, modes, 2 * modes)
+        return [shape(size, F32)] + [shape(size, BF16)] * n_send
+
     work = [pltpu.VMEM((2 * modes, depth), BF16), pltpu.VMEM((STRUCTS, modes, 2 * modes), F32)]
 
     ahead = routed(right_modes, "mode", lambda i: i - 1 if i % 2 == 0 else i - 3)
@@ -121,7 +133,7 @@
 
     rows, *group = pl.pallas_call(
         functools.partial(first_kernel, n_send),
-        out_shape=[shape((STRUCTS * modes, depth), BF16)] + outs,
+        out_shape=[shape((STRUCTS * modes, depth), BF16)] + outs(1),
         in_specs=[VMEM, VMEM, SMEM, SMEM, SMEM],
         out_specs=[VMEM] * (2 + n_send),
         scratch_shapes=[pltpu.VMEM((4 * STRUCTS, sites), F32)] * 3 + work,
@@ -129,19 +141,22 @@
         name="first",
     )(left_modes.reshape(modes, depth), right_modes.reshape(modes, depth), momenta.T, spin_perm.T, spin_phase.T)
     received = exchange(group)
-    for block in (ahead, swapped, far):
-        group = pl.pallas_call(
-            functools.partial(next_kernel, n_send),
-            out_shape=outs,
-            in_specs=[VMEM, VMEM],
+
+    def product(kernel, slots, block, *before):
+        return pl.pallas_call(
+            functools.partial(kernel, n_send),
+            out_shape=outs(slots),
+            in_specs=[VMEM] * (2 + len(before)),
             out_specs=[VMEM] * (1 + n_send),
             scratch_shapes=work,
             compiler_params=PARAMS,
-            name="next",
-        )(rows, block.reshape(modes, depth))
-        received += exchange(group)
+        )(rows, block.reshape(modes, depth), *before)
+
+    group = product(next_kernel, 1, ahead)
+    received += exchange(product(add_kernel, 2, swapped, *group))
+    received += exchange(product(next_kernel, 1, far))
     return pl.pallas_call(
-        functools.partial(join_kernel, CYCLE, 1.0 / math.sqrt(depth * spaces)),
+        functools.partial(join_kernel, spaces, 1.0 / math.sqrt(depth * spaces)),
         out_shape=shape((own * CYCLE * 2, modes, modes), F32),
         in_specs=[VMEM] * len(received),
         out_specs=VMEM,

time: 48.6 us -> 42.3 us (0.87)
  starting transfers between devices: 22.3 us -> 17.3 us
  waiting for transfers between devices: 15.1 us -> 13.8 us
    ppermute x15 -> x12, starting transfers between devices: 22.3 us -> 17.3 us  [routed(): lax.ppermute(block, axis, [(source(i) % size, i) for i in range(size)])]
    ppermute x15 -> x12, waiting for transfers between devices: 15.1 us -> 13.8 us  [routed(): lax.ppermute(block, axis, [(source(i) % size, i) for i in range(size)])]
  transfers between devices with their start and end apart: 15 -> 12, of which waited for: 4 -> 2; matrix products, arithmetic and copies ran while one was open for 5% -> 5% of each run, Pallas kernels for 12% -> 13%
where the time goes in v2:
time: 42.3 us; the launch traced here: 42.1 us
  starting transfers between devices  17.3 us (41%)
  waiting for transfers between devices  13.8 us (33%)
  Pallas kernels  6.55 us (15%)
  local copies, waits for them, and re-layouts  4.31 us (10%)
    ppermute x12, starting transfers between devices, routed(): lax.ppermute(block, axis, [(source(i) % size, i) for i in range(size)])  17.3 us
    ppermute x12, waiting for transfers between devices, routed(): lax.ppermute(block, axis, [(source(i) % size, i) for i in range(size)])  13.8 us
    unnamed x11, local copies, waits for them, and re-layouts  4.31 us
    pallas_call x3, Pallas kernels, product(): pl.pallas_call(functools.partial(kernel, n_send), out_shape=outs(slots),...  2.99 us
    pallas_call x1, Pallas kernels, local(): pl.pallas_call(functools.partial(first_kernel, n_send), out_shape=[shape(...  2.62 us
    pallas_call x1, Pallas kernels, local(): pl.pallas_call(functools.partial(join_kernel, spaces, 1.0 / math.sqrt(dep...  0.94 us
  transfers between devices with their start and end apart: 12, of which 2 were waited for; matrix products, arithmetic and copies ran while one was open for 5% of the time, Pallas kernels for 13%

profile of v2, /device:TPU:0, one launch (start us, length us, event | category | flops | bytes accessed | tf_op | source)
XLA Modules:
  0.0 42.1 jit_solution(1704014000779322658)
XLA Ops:
  0.0 2.4 %collective-permute-start.3 = (bf16[64,24,128]{2,1,0:T(8,128)(2,1)}, bf16[64,24,128]{2,1,0:T(8,128)(2,1)S(1)}, u32[]{:S(2)}, u32[]{:S(2)}) collective-permute-start(bf16[64,24,128]{2,1,0:T(8,128)(2,1)} %param.6), channel_id=1, source_target_pairs={{28,0},{24,4},{4,8},{0,12},{12,16},{8,20},{20,24},{16,28},{29,1},{... | collective-permute-start | bytes 1179656 | tf_op jit(solution)/shard_map/ppermute | solution.py:26
  2.4 0.7 %collective-permute-start.8 = (bf16[64,24,128]{2,1,0:T(8,128)(2,1)}, bf16[64,24,128]{2,1,0:T(8,128)(2,1)S(1)}, u32[]{:S(2)}, u32[]{:S(2)}) collective-permute-start(bf16[64,24,128]{2,1,0:T(8,128)(2,1)} %param.6), channel_id=1, source_target_pairs={{20,0},{0,4},{28,8},{8,12},{4,16},{16,20},{12,24},{24,28},{21,1},{... | collective-permute-start | bytes 1179656 | tf_op jit(solution)/shard_map/ppermute | solution.py:26
  3.1 9.4 %collective-permute-done.3 = bf16[64,24,128]{2,1,0:T(8,128)(2,1)S(1)} collective-permute-done((bf16[64,24,128]{2,1,0:T(8,128)(2,1)}, bf16[64,24,128]{2,1,0:T(8,128)(2,1)S(1)}, u32[]{:S(2)}, u32[]{:S(2)}) %collective-permute-start.3) | collective-permute-done | bytes 393248 | tf_op jit(solution)/shard_map/ppermute | solution.py:26
  12.5 0.7 %collective-permute-start.4 = (bf16[64,24,128]{2,1,0:T(8,128)(2,1)S(1)}, bf16[64,24,128]{2,1,0:T(8,128)(2,1)S(1)}, u32[]{:S(2)}, u32[]{:S(2)}) collective-permute-start(bf16[64,24,128]{2,1,0:T(8,128)(2,1)S(1)} %collective-permute-done.3), channel_id=1, source_target_pairs={{4,0},{0,4},{12,8},{8,12},{20,16},{16,20},{28,24},{24,28},{5,1},{1... | collective-permute-start | bytes 1179656 | tf_op jit(solution)/shard_map/ppermute | solution.py:26
  13.2 1.1 %copy.19 = bf16[8,8,24,128]{3,1,2,0:T(8,128)(2,1)S(1)} copy(bf16[8,8,24,128]{3,2,1,0:T(8,128)(2,1)} %bitcast.32) | data formatting | bytes 786432
  14.2 1.1 %copy.20 = bf16[8,8,24,128]{3,1,2,0:T(8,128)(2,1)S(1)} copy(bf16[8,8,24,128]{3,2,1,0:T(8,128)(2,1)} %bitcast.31) | data formatting | bytes 786432
  15.3 0.7 %copy-done = s32[8,3]{0,1:T(4,128)S(1)} copy-done((s32[8,3]{0,1:T(4,128)S(1)}, s32[8,3]{0,1:T(4,128)}, u32[]{:S(2)}) %copy-start) | copy-done | bytes 120
  16.0 0.7 %copy-done.1 = s32[8,4]{0,1:T(4,128)S(1)} copy-done((s32[8,4]{0,1:T(4,128)S(1)}, s32[8,4]{0,1:T(4,128)}, u32[]{:S(2)}) %copy-start.1) | copy-done | bytes 152
  16.7 0.7 %copy-done.2 = s32[8,4]{0,1:T(4,128)S(1)} copy-done((s32[8,4]{0,1:T(4,128)S(1)}, s32[8,4]{0,1:T(4,128)}, u32[]{:S(2)}) %copy-start.2) | copy-done | bytes 152
  17.3 2.6 %first.1 = (bf16[512,3072]{1,0:T(8,128)(2,1)S(1)}, f32[1,2,64,128]{3,2,1,0:T(8,128)S(1)}, bf16[1,2,64,128]{3,2,1,0:T(8,128)(2,1)S(1)}, bf16[1,2,64,128]{3,2,1,0:T(8,128)(2,1)S(1)}, bf16[1,2,64,128]{3,2,1,0:T(8,128)(2,1)S(1)}) custom-call(bf16[64,3072]{1,0:T(8,128)(2,1)S(1)} %bitcast.27, bf16[64,3072]{1,0:T(8,128)(2,1)S(1)} %bitcast.26, s32[3,8]{1,0:T(4,128)S(1)} %bitcast.28, ...), custom_call_target="tpu_custom_call" | custom-call | tf_op jit(solution)/shard_map/first/pallas_call | solution.py:134
  20.0 2.5 %collective-permute-start = (bf16[1,2,64,128]{3,2,1,0:T(8,128)(2,1)S(1)}, bf16[1,2,64,128]{3,2,1,0:T(8,128)(2,1)S(1)}, u32[]{:S(2)}, u32[]{:S(2)}) collective-permute-start(bf16[1,2,64,128]{3,2,1,0:T(8,128)(2,1)S(1)} %get-tuple-element.23), channel_id=1, source_target_pairs={{1,0},{0,1},{3,2},{2,3},{5,4},{4,5},{7,6},{6,7},{9,8},{8,9},{11,10... | collective-permute-start | bytes 98312 | tf_op jit(solution)/shard_map/ppermute | solution.py:26
  22.5 2.6 %collective-permute-start.1 = (bf16[1,2,64,128]{3,2,1,0:T(8,128)(2,1)S(1)}, bf16[1,2,64,128]{3,2,1,0:T(8,128)(2,1)S(1)}, u32[]{:S(2)}, u32[]{:S(2)}) collective-permute-start(bf16[1,2,64,128]{3,2,1,0:T(8,128)(2,1)S(1)} %get-tuple-element.24), channel_id=1, source_target_pairs={{2,0},{3,1},{0,2},{1,3},{6,4},{7,5},{4,6},{5,7},{10,8},{11,9},{8,1... | collective-permute-start | bytes 98312 | tf_op jit(solution)/shard_map/ppermute | solution.py:26
  25.1 0.1 copy.17
  25.2 0.1 copy.16
  25.2 1.0 %shard_map.55 = (f32[1,2,64,128]{3,2,1,0:T(8,128)S(1)}, bf16[1,2,64,128]{3,2,1,0:T(8,128)(2,1)S(1)}, bf16[1,2,64,128]{3,2,1,0:T(8,128)(2,1)S(1)}, bf16[1,2,64,128]{3,2,1,0:T(8,128)(2,1)S(1)}) custom-call(bf16[512,3072]{1,0:T(8,128)(2,1)S(1)} %get-tuple-element.26.rows, bf16[64,3072]{1,0:T(8,128)(2,1)S(1)} %bitcast.25), custom_call_target="tpu_custom_call" | custom-call | tf_op jit(solution)/shard_map/pallas_call | solution.py:146
  26.2 1.0 %shard_map.57 = (f32[1,2,64,128]{3,2,1,0:T(8,128)S(1)}, bf16[1,2,64,128]{3,2,1,0:T(8,128)(2,1)S(1)}, bf16[1,2,64,128]{3,2,1,0:T(8,128)(2,1)S(1)}, bf16[1,2,64,128]{3,2,1,0:T(8,128)(2,1)S(1)}) custom-call(bf16[512,3072]{1,0:T(8,128)(2,1)S(1)} %get-tuple-element.26.rows, bf16[64,3072]{1,0:T(8,128)(2,1)S(1)} %bitcast.23), custom_call_target="tpu_custom_call" | custom-call | tf_op jit(solution)/shard_map/pallas_call | solution.py:146
  27.2 2.0 %collective-permute-start.10 = (bf16[1,2,64,128]{3,2,1,0:T(8,128)(2,1)S(1)}, bf16[1,2,64,128]{3,2,1,0:T(8,128)(2,1)S(1)}, u32[]{:S(2)}, u32[]{:S(2)}) collective-permute-start(bf16[1,2,64,128]{3,2,1,0:T(8,128)(2,1)S(1)} %get-tuple-element.37), channel_id=1, source_target_pairs={{2,0},{3,1},{0,2},{1,3},{6,4},{7,5},{4,6},{5,7},{10,8},{11,9},{8,1... | collective-permute-start | bytes 98312 | tf_op jit(solution)/shard_map/ppermute | solution.py:26
  29.2 0.1 copy.18
  29.3 1.0 %shard_map.56 = (f32[2,2,64,128]{3,2,1,0:T(8,128)S(1)}, bf16[2,2,64,128]{3,2,1,0:T(8,128)(2,1)S(1)}, bf16[2,2,64,128]{3,2,1,0:T(8,128)(2,1)S(1)}, bf16[2,2,64,128]{3,2,1,0:T(8,128)(2,1)S(1)}) custom-call(bf16[512,3072]{1,0:T(8,128)(2,1)S(1)} %get-tuple-element.26.rows, bf16[64,3072]{1,0:T(8,128)(2,1)S(1)} %bitcast.24, ...), custom_call_target="tpu_custom_call" | custom-call | tf_op jit(solution)/shard_map/pallas_call | solution.py:146
  30.3 2.6 %collective-permute-start.5 = (bf16[2,2,64,128]{3,2,1,0:T(8,128)(2,1)S(1)}, bf16[2,2,64,128]{3,2,1,0:T(8,128)(2,1)S(1)}, u32[]{:S(2)}, u32[]{:S(2)}) collective-permute-start(bf16[2,2,64,128]{3,2,1,0:T(8,128)(2,1)S(1)} %get-tuple-element.32), channel_id=1, source_target_pairs={{1,0},{0,1},{3,2},{2,3},{5,4},{4,5},{7,6},{6,7},{9,8},{8,9},{11,10... | collective-permute-start | bytes 196616 | tf_op jit(solution)/shard_map/ppermute | solution.py:26
  32.9 2.4 %collective-permute-start.7 = (bf16[2,2,64,128]{3,2,1,0:T(8,128)(2,1)S(1)}, bf16[2,2,64,128]{3,2,1,0:T(8,128)(2,1)S(1)}, u32[]{:S(2)}, u32[]{:S(2)}) collective-permute-start(bf16[2,2,64,128]{3,2,1,0:T(8,128)(2,1)S(1)} %get-tuple-element.34), channel_id=1, source_target_pairs={{3,0},{2,1},{1,2},{0,3},{7,4},{6,5},{5,6},{4,7},{11,8},{10,9},{9,1... | collective-permute-start | bytes 196616 | tf_op jit(solution)/shard_map/ppermute | solution.py:26
  35.3 1.4 %collective-permute-start.11 = (bf16[1,2,64,128]{3,2,1,0:T(8,128)(2,1)S(1)}, bf16[1,2,64,128]{3,2,1,0:T(8,128)(2,1)S(1)}, u32[]{:S(2)}, u32[]{:S(2)}) collective-permute-start(bf16[1,2,64,128]{3,2,1,0:T(8,128)(2,1)S(1)} %get-tuple-element.38), channel_id=1, source_target_pairs={{3,0},{2,1},{1,2},{0,3},{7,4},{6,5},{5,6},{4,7},{11,8},{10,9},{9,1... | collective-permute-start | bytes 98312 | tf_op jit(solution)/shard_map/ppermute | solution.py:26
  36.8 4.4 %collective-permute-done.11.refs_11_ = bf16[1,2,64,128]{3,2,1,0:T(8,128)(2,1)S(1)} collective-permute-done((bf16[1,2,64,128]{3,2,1,0:T(8,128)(2,1)S(1)}, bf16[1,2,64,128]{3,2,1,0:T(8,128)(2,1)S(1)}, u32[]{:S(2)}, u32[]{:S(2)}) %collective-permute-start.11) | collective-permute-done | bytes 32800 | tf_op jit(solution)/shard_map/ppermute | solution.py:26
  41.1 0.9 %join.1 = f32[16,64,64]{2,1,0:T(8,128)} custom-call(f32[1,2,64,128]{3,2,1,0:T(8,128)S(1)} %get-tuple-element.22.refs_0_, bf16[1,2,64,128]{3,2,1,0:T(8,128)(2,1)S(1)} %collective-permute-done.refs_1_, bf16[1,2,64,128]{3,2,1,0:T(8,128)(2,1)S(1)} %collective-permute-done.1.refs_2_, bf16[1,2,64,128]{3,2,1,0:T(8,128)(2,1)S(1)} %collective-permute-done.2.refs_3_, ...), custom_call_target="tpu_custom_call" | custom-call | tf_op jit(solution)/shard_map/join/pallas_call | solution.py:158
  (16 shorter events, 0.1 us)
Async XLA Ops:
  0.0 12.5 %collective-permute-start.3 = (bf16[64,24,128]{2,1,0:T(8,128)(2,1)}, bf16[64,24,128]{2,1,0:T(8,128)(2,1)S(1)}, u32[]{:S(2)}, u32[]{:S(2)}) collective-permute-start(bf16[64,24,128]{2,1,0:T(8,128)(2,1)} %param.6), channel_id=1, source_target_pairs={{28,0},{24,4},{4,8},{0,12},{12,16},{8,20},{20,24},{16,28},{29,1},{... | collective-permute-start | bytes 1179656 | tf_op jit(solution)/shard_map/ppermute | solution.py:26
  2.4 22.8 %collective-permute-start.8 = (bf16[64,24,128]{2,1,0:T(8,128)(2,1)}, bf16[64,24,128]{2,1,0:T(8,128)(2,1)S(1)}, u32[]{:S(2)}, u32[]{:S(2)}) collective-permute-start(bf16[64,24,128]{2,1,0:T(8,128)(2,1)} %param.6), channel_id=1, source_target_pairs={{20,0},{0,4},{28,8},{8,12},{4,16},{16,20},{12,24},{24,28},{21,1},{... | collective-permute-start | bytes 1179656 | tf_op jit(solution)/shard_map/ppermute | solution.py:26
  12.5 16.7 %collective-permute-start.4 = (bf16[64,24,128]{2,1,0:T(8,128)(2,1)S(1)}, bf16[64,24,128]{2,1,0:T(8,128)(2,1)S(1)}, u32[]{:S(2)}, u32[]{:S(2)}) collective-permute-start(bf16[64,24,128]{2,1,0:T(8,128)(2,1)S(1)} %collective-permute-done.3), channel_id=1, source_target_pairs={{4,0},{0,4},{12,8},{8,12},{20,16},{16,20},{28,24},{24,28},{5,1},{1... | collective-permute-start | bytes 1179656 | tf_op jit(solution)/shard_map/ppermute | solution.py:26
  15.3 0.7 %copy-start = (s32[8,3]{0,1:T(4,128)S(1)}, s32[8,3]{0,1:T(4,128)}, u32[]{:S(2)}) copy-start(s32[8,3]{0,1:T(4,128)} %param.7) | copy-start | bytes 292
  16.0 0.7 %copy-start.1 = (s32[8,4]{0,1:T(4,128)S(1)}, s32[8,4]{0,1:T(4,128)}, u32[]{:S(2)}) copy-start(s32[8,4]{0,1:T(4,128)} %param.8) | copy-start | bytes 388
  16.7 0.7 %copy-start.2 = (s32[8,4]{0,1:T(4,128)S(1)}, s32[8,4]{0,1:T(4,128)}, u32[]{:S(2)}) copy-start(s32[8,4]{0,1:T(4,128)} %param.9) | copy-start | bytes 388
  20.0 12.9 %collective-permute-start = (bf16[1,2,64,128]{3,2,1,0:T(8,128)(2,1)S(1)}, bf16[1,2,64,128]{3,2,1,0:T(8,128)(2,1)S(1)}, u32[]{:S(2)}, u32[]{:S(2)}) collective-permute-start(bf16[1,2,64,128]{3,2,1,0:T(8,128)(2,1)S(1)} %get-tuple-element.23), channel_id=1, source_target_pairs={{1,0},{0,1},{3,2},{2,3},{5,4},{4,5},{7,6},{6,7},{9,8},{8,9},{11,10... | collective-permute-start | bytes 98312 | tf_op jit(solution)/shard_map/ppermute | solution.py:26
  22.5 10.4 %collective-permute-start.1 = (bf16[1,2,64,128]{3,2,1,0:T(8,128)(2,1)S(1)}, bf16[1,2,64,128]{3,2,1,0:T(8,128)(2,1)S(1)}, u32[]{:S(2)}, u32[]{:S(2)}) collective-permute-start(bf16[1,2,64,128]{3,2,1,0:T(8,128)(2,1)S(1)} %get-tuple-element.24), channel_id=1, source_target_pairs={{2,0},{3,1},{0,2},{1,3},{6,4},{7,5},{4,6},{5,7},{10,8},{11,9},{8,1... | collective-permute-start | bytes 98312 | tf_op jit(solution)/shard_map/ppermute | solution.py:26
  25.1 10.2 %collective-permute-start.2 = (bf16[1,2,64,128]{3,2,1,0:T(8,128)(2,1)S(1)}, bf16[1,2,64,128]{3,2,1,0:T(8,128)(2,1)S(1)}, u32[]{:S(2)}, u32[]{:S(2)}) collective-permute-start(bf16[1,2,64,128]{3,2,1,0:T(8,128)(2,1)S(1)} %get-tuple-element.25), channel_id=1, source_target_pairs={{3,0},{2,1},{1,2},{0,3},{7,4},{6,5},{5,6},{4,7},{11,8},{10,9},{9,1... | collective-permute-start | bytes 98312 | tf_op jit(solution)/shard_map/ppermute | solution.py:26
  27.2 9.5 %collective-permute-start.10 = (bf16[1,2,64,128]{3,2,1,0:T(8,128)(2,1)S(1)}, bf16[1,2,64,128]{3,2,1,0:T(8,128)(2,1)S(1)}, u32[]{:S(2)}, u32[]{:S(2)}) collective-permute-start(bf16[1,2,64,128]{3,2,1,0:T(8,128)(2,1)S(1)} %get-tuple-element.37), channel_id=1, source_target_pairs={{2,0},{3,1},{0,2},{1,3},{6,4},{7,5},{4,6},{5,7},{10,8},{11,9},{8,1... | collective-permute-start | bytes 98312 | tf_op jit(solution)/shard_map/ppermute | solution.py:26
  30.3 10.9 %collective-permute-start.5 = (bf16[2,2,64,128]{3,2,1,0:T(8,128)(2,1)S(1)}, bf16[2,2,64,128]{3,2,1,0:T(8,128)(2,1)S(1)}, u32[]{:S(2)}, u32[]{:S(2)}) collective-permute-start(bf16[2,2,64,128]{3,2,1,0:T(8,128)(2,1)S(1)} %get-tuple-element.32), channel_id=1, source_target_pairs={{1,0},{0,1},{3,2},{2,3},{5,4},{4,5},{7,6},{6,7},{9,8},{8,9},{11,10... | collective-permute-start | bytes 196616 | tf_op jit(solution)/shard_map/ppermute | solution.py:26
  32.9 8.3 %collective-permute-start.6 = (bf16[2,2,64,128]{3,2,1,0:T(8,128)(2,1)S(1)}, bf16[2,2,64,128]{3,2,1,0:T(8,128)(2,1)S(1)}, u32[]{:S(2)}, u32[]{:S(2)}) collective-permute-start(bf16[2,2,64,128]{3,2,1,0:T(8,128)(2,1)S(1)} %get-tuple-element.33), channel_id=1, source_target_pairs={{2,0},{3,1},{0,2},{1,3},{6,4},{7,5},{4,6},{5,7},{10,8},{11,9},{8,1... | collective-permute-start | bytes 196616 | tf_op jit(solution)/shard_map/ppermute | solution.py:26
  32.9 8.2 %collective-permute-start.7 = (bf16[2,2,64,128]{3,2,1,0:T(8,128)(2,1)S(1)}, bf16[2,2,64,128]{3,2,1,0:T(8,128)(2,1)S(1)}, u32[]{:S(2)}, u32[]{:S(2)}) collective-permute-start(bf16[2,2,64,128]{3,2,1,0:T(8,128)(2,1)S(1)} %get-tuple-element.34), channel_id=1, source_target_pairs={{3,0},{2,1},{1,2},{0,3},{7,4},{6,5},{5,6},{4,7},{11,8},{10,9},{9,1... | collective-permute-start | bytes 196616 | tf_op jit(solution)/shard_map/ppermute | solution.py:26
  35.3 5.8 %collective-permute-start.11 = (bf16[1,2,64,128]{3,2,1,0:T(8,128)(2,1)S(1)}, bf16[1,2,64,128]{3,2,1,0:T(8,128)(2,1)S(1)}, u32[]{:S(2)}, u32[]{:S(2)}) collective-permute-start(bf16[1,2,64,128]{3,2,1,0:T(8,128)(2,1)S(1)} %get-tuple-element.38), channel_id=1, source_target_pairs={{3,0},{2,1},{1,2},{0,3},{7,4},{6,5},{5,6},{4,7},{11,8},{10,9},{9,1... | collective-permute-start | bytes 98312 | tf_op jit(solution)/shard_map/ppermute | solution.py:26
  36.8 4.4 %collective-permute-start.9 = (bf16[1,2,64,128]{3,2,1,0:T(8,128)(2,1)S(1)}, bf16[1,2,64,128]{3,2,1,0:T(8,128)(2,1)S(1)}, u32[]{:S(2)}, u32[]{:S(2)}) collective-permute-start(bf16[1,2,64,128]{3,2,1,0:T(8,128)(2,1)S(1)} %get-tuple-element.36), channel_id=1, source_target_pairs={{1,0},{0,1},{3,2},{2,3},{5,4},{4,5},{7,6},{6,7},{9,8},{8,9},{11,10... | collective-permute-start | bytes 98312 | tf_op jit(solution)/shard_map/ppermute | solution.py:26

commit v3 on v1

--- a/solution.py
+++ b/solution.py
@@ -17,7 +17,7 @@
 F32 = jnp.float32
 BF16 = jnp.bfloat16
 VMEM = pl.BlockSpec(memory_space=pltpu.VMEM)
-SMEM = pl.BlockSpec(memory_space=pltpu.SMEM)
+HBM = pl.BlockSpec(memory_space=pltpu.HBM)
 PARAMS = pltpu.CompilerParams(vmem_limit_bytes=16 << 20)
 
 
@@ -26,16 +26,13 @@
     return lax.ppermute(block, axis, [(source(i) % size, i) for i in range(size)])
 
 
-def build_rows(left, momenta, perm, phase, angle, cosine, sine, rows):
-    modes = left.shape[0]
-    structs = momenta.shape[1]
-    sites = left.shape[1] // 24
-    half = 12 * sites
+def turn_tables(momenta, phase, angle, cosine, sine):
+    sites = angle.shape[1]
     site = lax.axis_index("space") * sites + lax.broadcasted_iota(jnp.int32, (1, sites), 1)
     x = (site % BOX).astype(F32)
     y = (site // BOX % BOX).astype(F32)
     z = (site // (BOX * BOX)).astype(F32)
-    for g in range(structs):
+    for g in range(momenta.shape[1]):
         dot = momenta[0, g].astype(F32) * x + momenta[1, g].astype(F32) * y + momenta[2, g].astype(F32) * z
         for a in range(4):
             angle[g * 4 + a : g * 4 + a + 1, :] = (LAT // 4 * phase[a, g]).astype(F32) - dot
@@ -44,12 +41,18 @@
     psi = steps * (2.0 * math.pi / LAT)
     cosine[...] = jnp.cos(psi)
     sine[...] = jnp.sin(psi)
+
+
+def turn_rows(left, perm, cosine, sine, rows):
+    modes = left.shape[0]
+    sites = cosine.shape[1]
+    half = 12 * sites
     for a in range(4):
         for k in range(3):
             at = (a * 3 + k) * sites
             re = left[:, at : at + sites].astype(F32)
             im = left[:, half + at : half + at + sites].astype(F32)
-            for g in range(structs):
+            for g in range(perm.shape[1]):
                 co = cosine[g * 4 + a : g * 4 + a + 1, :]
                 si = sine[g * 4 + a : g * 4 + a + 1, :]
                 to = pl.multiple_of((perm[a, g] * 3 + k) * sites, LANES)
@@ -58,47 +61,91 @@
                 rows[g * modes : (g + 1) * modes, pl.ds(to, sites)] = (im * co - re * si).astype(BF16)
 
 
-def multiply(rows, right, both, total, sends, kept):
+def flatten(block, flat):
+    for at in range(0, block.shape[0], 16):
+        flat[at : at + 16, :] = block[at : at + 16].reshape(16, flat.shape[1])
+
+
+def multiply(all_rows, right, both, total, kept, sends):
     modes, depth = right.shape
     half = depth // 2
     both[0:modes, :] = right[...]
     both[modes:, 0:half] = right[:, half:]
     both[modes:, half:] = -right[:, 0:half]
-    total[...] = lax.dot_general(
-        rows[...], both[...], (((1,), (1,)), ((), ())), preferred_element_type=F32
-    ).reshape(total.shape)
     me = lax.axis_index("space")
-    own = kept.shape[0]
-    kept[...] = total[pl.ds(me * own, own)]
-    for distance, send in enumerate(sends, 1):
-        send[...] = total[pl.ds((me ^ distance) * own, own)].astype(BF16)
-
-
-def first_kernel(n_send, left, right, momenta, perm, phase, rows, kept, *rest):
-    sends, (angle, cosine, sine, both, total) = rest[:n_send], rest[n_send:]
-    build_rows(left, momenta, perm, phase, angle, cosine, sine, rows)
-    multiply(rows, right, both, total, sends, kept)
-
-
-def next_kernel(n_send, rows, right, kept, *rest):
-    sends, (both, total) = rest[:n_send], rest[n_send:]
-    multiply(rows, right, both, total, sends, kept)
-
-
-def join_kernel(groups, factor, *refs):
-    out = refs[-1]
-    each = (len(refs) - 1) // groups
+    own = kept.shape[1]
+    for slot, rows in enumerate(all_rows):
+        total[...] = lax.dot_general(
+            rows[...], both[...], (((1,), (1,)), ((), ())), preferred_element_type=F32
+        ).reshape(total.shape)
+        kept[slot] = total[pl.ds(me * own, own)]
+        for distance, send in enumerate(sends, 1):
+            send[slot] = total[pl.ds((me ^ distance) * own, own)].astype(BF16)
+
+
+def first_kernel(n_send, left, right, momenta, perm, phase, rows, cosine, sine, kept, *rest):
+    sends, (both, total, angle, lefts, rights, flat, *tables, done) = rest[:n_send], rest[n_send:]
+    pairs = list(zip((momenta, perm, phase, left, right), (*tables, lefts, rights)))
+    copies = [pltpu.make_async_copy(source, target, done.at[i]) for i, (source, target) in enumerate(pairs)]
+    for copy in copies:
+        copy.start()
+    for copy in copies[:-1]:
+        copy.wait()
+    turn_tables(tables[0], tables[2], angle, cosine, sine)
+    flatten(lefts, flat)
+    turn_rows(flat, tables[1], cosine, sine, rows)
+    copies[-1].wait()
+    flatten(rights, flat)
+    multiply((rows,), flat, both, total, kept, sends)
+
+
+def other_kernel(left, perm, cosine, sine, rows, flat, table, done):
+    copy = pltpu.make_async_copy(perm, table, done)
+    copy.start()
+    flatten(left, flat)
+    copy.wait()
+    turn_rows(flat, table, cosine, sine, rows)
+
+
+def product_kernel(n_rows, *refs):
+    all_rows, (right, kept, *sends, both, total) = refs[:n_rows], refs[n_rows:]
+    multiply(all_rows, right, both, total, kept, sends)
+
+
+def summed(parts, slot, g, factor):
+    value = parts[0][slot, g]
+    for part in parts[1:]:
+        value = value + part[slot, g].astype(F32)
+    return value * factor
+
+
+def join_kernel(spaces, factor, *refs):
+    early, middle, (out, other) = refs[:spaces], refs[spaces : 2 * spaces], refs[2 * spaces :]
     odd = lax.axis_index("mode") % 2
-    places = (0, 1 + 2 * odd, 2, 3 - 2 * odd)
     modes = out.shape[1]
-    for place, start in zip(places, range(0, groups * each, each)):
-        for g in range(refs[start].shape[0]):
-            value = refs[start][g]
-            for part in refs[start + 1 : start + each]:
-                value = value + part[g].astype(F32)
-            value = value * factor
+    for g in range(other.shape[0]):
+        other[g] = summed(middle, 1, g, factor)
+        for parts, place in ((early, 0), (middle, 1 + 2 * odd)):
+            value = summed(parts, 0, g, factor)
             for p in range(2):
                 out[(g * CYCLE + place) * 2 + p] = value[:, p * modes : (p + 1) * modes]
+
+
+def last_kernel(factor, swapped, *refs):
+    late, (_, out, planes, done) = refs[:-4], refs[-4:]
+    odd = lax.axis_index("mode") % 2
+    modes = out.shape[1]
+    copies = []
+    for g in range(swapped.shape[0]):
+        for n, place in enumerate((2, 3 - 2 * odd)):
+            value = swapped[g] if n == 0 else summed(late, 0, g, factor)
+            for p in range(2):
+                planes[g, n, p] = value[:, p * modes : (p + 1) * modes]
+            to = out.at[pl.ds((g * CYCLE + place) * 2, 2)]
+            copies.append(pltpu.make_async_copy(planes.at[g, n], to, done.at[2 * g + n]))
+            copies[-1].start()
+    for copy in copies:
+        copy.wait()
 
 
 def local(left_modes, right_modes, momenta, spin_perm, spin_phase):
@@ -108,46 +155,84 @@
     own = STRUCTS // spaces
     n_send = spaces - 1
     shape = jax.ShapeDtypeStruct
-    outs = [shape((own, modes, 2 * modes), F32)] + [shape((own, modes, 2 * modes), BF16)] * n_send
+
+    def outs(slots):
+        size = (slots, own, modes, 2 * modes)
+        return [shape(size, F32)] + [shape(size, BF16)] * n_send
+
     work = [pltpu.VMEM((2 * modes, depth), BF16), pltpu.VMEM((STRUCTS, modes, 2 * modes), F32)]
 
     ahead = routed(right_modes, "mode", lambda i: i - 1 if i % 2 == 0 else i - 3)
+    other_left = routed(left_modes, "mode", lambda i: i ^ 1)
     far = routed(right_modes, "mode", lambda i: i - 3 if i % 2 == 0 else i - 1)
-    swapped = routed(ahead, "mode", lambda i: i ^ 1)
+    in_hbm = [pltpu.with_memory_space_constraint(t, pltpu.HBM) for t in (left_modes, right_modes)]
+    tables = [pltpu.with_memory_space_constraint(t.T, pltpu.HBM) for t in (momenta, spin_perm, spin_phase)]
+    table_shapes = [pltpu.SMEM(t.shape, jnp.int32) for t in tables]
+    flat = pltpu.VMEM((modes, depth), BF16)
+    rows_shape = shape((STRUCTS * modes, depth), BF16)
+    turn_shape = shape((4 * STRUCTS, sites), F32)
 
     def exchange(group):
         kept, *sends = group
         return [kept] + [routed(s, "space", lambda i, d=d: i ^ d) for d, s in enumerate(sends, 1)]
 
-    rows, *group = pl.pallas_call(
-        functools.partial(first_kernel, n_send),
-        out_shape=[shape((STRUCTS * modes, depth), BF16)] + outs,
-        in_specs=[VMEM, VMEM, SMEM, SMEM, SMEM],
-        out_specs=[VMEM] * (2 + n_send),
-        scratch_shapes=[pltpu.VMEM((4 * STRUCTS, sites), F32)] * 3 + work,
-        compiler_params=PARAMS,
-        name="first",
-    )(left_modes.reshape(modes, depth), right_modes.reshape(modes, depth), momenta.T, spin_perm.T, spin_phase.T)
-    received = exchange(group)
-    for block in (ahead, swapped, far):
-        group = pl.pallas_call(
-            functools.partial(next_kernel, n_send),
-            out_shape=outs,
-            in_specs=[VMEM, VMEM],
-            out_specs=[VMEM] * (1 + n_send),
+    def product(all_rows, block):
+        return pl.pallas_call(
+            functools.partial(product_kernel, len(all_rows)),
+            out_shape=outs(len(all_rows)),
+            in_specs=[VMEM] * (len(all_rows) + 1),
+            out_specs=[VMEM] * spaces,
             scratch_shapes=work,
             compiler_params=PARAMS,
-            name="next",
-        )(rows, block.reshape(modes, depth))
-        received += exchange(group)
+        )(*all_rows, block.reshape(modes, depth))
+
+    rows, cosine, sine, *group = pl.pallas_call(
+        functools.partial(first_kernel, n_send),
+        out_shape=[rows_shape, turn_shape, turn_shape] + outs(1),
+        in_specs=[HBM] * 5,
+        out_specs=[VMEM] * (3 + spaces),
+        scratch_shapes=work
+        + [pltpu.VMEM(turn_shape.shape, F32)]
+        + [pltpu.VMEM(left_modes.shape, BF16)] * 2
+        + [flat]
+        + table_shapes
+        + [pltpu.SemaphoreType.DMA((5,))],
+        compiler_params=PARAMS,
+        name="first",
+    )(*in_hbm, *tables)
+    early = exchange(group)
+    other_rows = pl.pallas_call(
+        other_kernel,
+        out_shape=rows_shape,
+        in_specs=[VMEM, HBM, VMEM, VMEM],
+        out_specs=VMEM,
+        scratch_shapes=[flat, table_shapes[1], pltpu.SemaphoreType.DMA],
+        compiler_params=PARAMS,
+        name="other",
+    )(other_left, tables[1], cosine, sine)
+    middle = exchange(product((rows, other_rows), ahead))
+    late = exchange(product((rows,), far))
+    factor = 1.0 / math.sqrt(depth * spaces)
+    result = shape((own * CYCLE * 2, modes, modes), F32)
+    out, other = pl.pallas_call(
+        functools.partial(join_kernel, spaces, factor),
+        out_shape=[result, shape((own, modes, 2 * modes), F32)],
+        in_specs=[VMEM] * (2 * spaces),
+        out_specs=[VMEM] * 2,
+        compiler_params=PARAMS,
+        name="join",
+    )(*early, *middle)
+    swapped = routed(other, "mode", lambda i: i ^ 1)
     return pl.pallas_call(
-        functools.partial(join_kernel, CYCLE, 1.0 / math.sqrt(depth * spaces)),
-        out_shape=shape((own * CYCLE * 2, modes, modes), F32),
-        in_specs=[VMEM] * len(received),
-        out_specs=VMEM,
-        compiler_params=PARAMS,
-        name="join",
-    )(*received)
+        functools.partial(last_kernel, factor),
+        out_shape=result,
+        in_specs=[VMEM] * (1 + spaces) + [HBM],
+        out_specs=HBM,
+        scratch_shapes=[pltpu.VMEM((own, 2, 2, modes, modes), F32), pltpu.SemaphoreType.DMA((2 * own,))],
+        input_output_aliases={1 + spaces: 0},
+        compiler_params=PARAMS,
+        name="last",
+    )(swapped, *late, out)
 
 
 def turned_rows(mode_rows, momenta, spin_perm, spin_phase, coords, struct_id):

time: 48.6 us -> 40.9 us (0.84)
  waiting for transfers between devices: 15.1 us -> 9.67 us
  local copies, waits for them, and re-layouts: 4.31 us -> 0.11 us
  Pallas kernels: 6.54 us -> 9.47 us
  starting transfers between devices: 22.3 us -> 21.4 us
    ppermute x15 -> x13, waiting for transfers between devices: 15.1 us -> 9.67 us  [routed(): lax.ppermute(block, axis, [(source(i) % size, i) for i in range(size)])]
    unnamed x11 -> x2, local copies, waits for them, and re-layouts: 4.31 us -> 0.11 us
    pallas_call x5 -> x6, Pallas kernels: 6.54 us -> 9.47 us  [the longest x1 3.21 us: local(): pl.pallas_call(functools.partial(first_kernel, n_send), out_shape=[rows_s...]
    ppermute x15 -> x13, starting transfers between devices: 22.3 us -> 21.4 us  [routed(): lax.ppermute(block, axis, [(source(i) % size, i) for i in range(size)])]
  transfers between devices with their start and end apart: 15 -> 13, of which waited for: 4 -> 4; matrix products, arithmetic and copies ran while one was open for 5% -> 0% of each run, Pallas kernels for 12% -> 21%
where the time goes in v3:
time: 40.9 us; the launch traced here: 40.7 us
  starting transfers between devices  21.4 us (52%)
  waiting for transfers between devices  9.67 us (24%)
  Pallas kernels  9.47 us (23%)
    ppermute x13, starting transfers between devices, routed(): lax.ppermute(block, axis, [(source(i) % size, i) for i in range(size)])  21.4 us
    ppermute x13, waiting for transfers between devices, routed(): lax.ppermute(block, axis, [(source(i) % size, i) for i in range(size)])  9.67 us
    pallas_call x1, Pallas kernels, local(): pl.pallas_call(functools.partial(first_kernel, n_send), out_shape=[rows_s...  3.21 us
    pallas_call x2, Pallas kernels, product(): pl.pallas_call(functools.partial(product_kernel, len(all_rows)), out_shap...  2.82 us
    pallas_call x1, Pallas kernels, local(): pl.pallas_call(other_kernel, out_shape=rows_shape, in_specs=[VMEM, HBM, V...  1.73 us
    pallas_call x1, Pallas kernels, local(): pl.pallas_call(functools.partial(join_kernel, spaces, factor), out_shape=...  0.9 us
  transfers between devices with their start and end apart: 13, of which 4 were waited for; matrix products, arithmetic and copies ran while one was open for 0% of the time, Pallas kernels for 21%

profile of v3, /device:TPU:0, one launch (start us, length us, event | category | flops | bytes accessed | tf_op | source)
XLA Modules:
  0.0 40.7 jit_solution(5141775188542275283)
XLA Ops:
  0.0 2.4 %collective-permute-start.4 = (bf16[64,24,128]{2,1,0:T(8,128)(2,1)}, bf16[64,24,128]{2,1,0:T(8,128)(2,1)S(1)}, u32[]{:S(2)}, u32[]{:S(2)}) collective-permute-start(bf16[64,24,128]{2,1,0:T(8,128)(2,1)} %right.1), channel_id=1, source_target_pairs={{28,0},{24,4},{4,8},{0,12},{12,16},{8,20},{20,24},{16,28},{29,1},{... | collective-permute-start | bytes 1179656 | tf_op jit(solution)/shard_map/ppermute | solution.py:26
  2.4 0.7 %collective-permute-start.3 = (bf16[64,24,128]{2,1,0:T(8,128)(2,1)}, bf16[64,24,128]{2,1,0:T(8,128)(2,1)S(1)}, u32[]{:S(2)}, u32[]{:S(2)}) collective-permute-start(bf16[64,24,128]{2,1,0:T(8,128)(2,1)} %left.1), channel_id=1, source_target_pairs={{4,0},{0,4},{12,8},{8,12},{20,16},{16,20},{28,24},{24,28},{5,1},{1... | collective-permute-start | bytes 1179656 | tf_op jit(solution)/shard_map/ppermute | solution.py:26
  3.1 0.0 collective-permute-start.9
  3.1 3.2 %first.1 = (bf16[512,3072]{1,0:T(8,128)(2,1)S(1)}, f32[32,128]{1,0:T(8,128)S(1)}, f32[32,128]{1,0:T(8,128)S(1)}, f32[1,2,64,128]{3,2,1,0:T(8,128)S(1)}, bf16[1,2...) custom-call(bf16[64,24,128]{2,1,0:T(8,128)(2,1)} %left.1, ...), custom_call_target="tpu_custom_call" | custom-call | tf_op jit(solution)/shard_map/first/pallas_call | solution.py:189
  6.3 1.6 %collective-permute-start = (bf16[1,2,64,128]{3,2,1,0:T(8,128)(2,1)S(1)}, bf16[1,2,64,128]{3,2,1,0:T(8,128)(2,1)S(1)}, u32[]{:S(2)}, u32[]{:S(2)}) collective-permute-start(bf16[1,2,64,128]{3,2,1,0:T(8,128)(2,1)S(1)} %get-tuple-element.23), channel_id=1, source_target_pairs={{1,0},{0,1},{3,2},{2,3},{5,4},{4,5},{7,6},{6,7},{9,8},{8,9},{11,10... | collective-permute-start | bytes 98312 | tf_op jit(solution)/shard_map/ppermute | solution.py:26
  7.9 2.6 %collective-permute-start.1 = (bf16[1,2,64,128]{3,2,1,0:T(8,128)(2,1)S(1)}, bf16[1,2,64,128]{3,2,1,0:T(8,128)(2,1)S(1)}, u32[]{:S(2)}, u32[]{:S(2)}) collective-permute-start(bf16[1,2,64,128]{3,2,1,0:T(8,128)(2,1)S(1)} %get-tuple-element.24), channel_id=1, source_target_pairs={{2,0},{3,1},{0,2},{1,3},{6,4},{7,5},{4,6},{5,7},{10,8},{11,9},{8,1... | collective-permute-start | bytes 98312 | tf_op jit(solution)/shard_map/ppermute | solution.py:26
  10.6 1.9 %collective-permute-done.4 = bf16[64,24,128]{2,1,0:T(8,128)(2,1)S(1)} collective-permute-done((bf16[64,24,128]{2,1,0:T(8,128)(2,1)}, bf16[64,24,128]{2,1,0:T(8,128)(2,1)S(1)}, u32[]{:S(2)}, u32[]{:S(2)}) %collective-permute-start.4) | collective-permute-done | bytes 393248 | tf_op jit(solution)/shard_map/ppermute | solution.py:26
  12.5 0.1 copy.12
  12.6 1.7 %other.1.refs_1_ = bf16[512,3072]{1,0:T(8,128)(2,1)S(1)} custom-call(bf16[64,24,128]{2,1,0:T(8,128)(2,1)S(1)} %collective-permute-done.3.left, s32[4,8]{1,0:T(4,128)} %bitcast.16, f32[32,128]{1,0:T(8,128)S(1)} %get-tuple-element.27.cosine, f32[32,128]{1,0:T(8,128)S(1)} %get-tuple-element.28.sine), custom_call_target="tpu_custom_call" | custom-call | tf_op jit(solution)/shard_map/other/pallas_call | solution.py:204
  14.3 1.8 %shard_map.55 = (f32[2,2,64,128]{3,2,1,0:T(8,128)S(1)}, bf16[2,2,64,128]{3,2,1,0:T(8,128)(2,1)S(1)}, bf16[2,2,64,128]{3,2,1,0:T(8,128)(2,1)S(1)}, bf16[2,2,64,128]{3,2,1,0:T(8,128)(2,1)S(1)}) custom-call(bf16[512,3072]{1,0:T(8,128)(2,1)S(1)} %get-tuple-element.26.refs_0_, bf16[512,3072]{1,0:T(8,128)(2,1)S(1)} %other.1.refs_1_, bf16[64,3072]{1,0:T(8,128)(2,1)S(1)} %bitcast.11), custom_call_target="tpu_custom_call" | custom-call | tf_op jit(solution)/shard_map/pallas_call | solution.py:180
  16.1 3.1 %collective-permute-start.5 = (bf16[2,2,64,128]{3,2,1,0:T(8,128)(2,1)S(1)}, bf16[2,2,64,128]{3,2,1,0:T(8,128)(2,1)S(1)}, u32[]{:S(2)}, u32[]{:S(2)}) collective-permute-start(bf16[2,2,64,128]{3,2,1,0:T(8,128)(2,1)S(1)} %get-tuple-element.30), channel_id=1, source_target_pairs={{1,0},{0,1},{3,2},{2,3},{5,4},{4,5},{7,6},{6,7},{9,8},{8,9},{11,10... | collective-permute-start | bytes 196616 | tf_op jit(solution)/shard_map/ppermute | solution.py:26
  19.3 2.6 %collective-permute-start.6 = (bf16[2,2,64,128]{3,2,1,0:T(8,128)(2,1)S(1)}, bf16[2,2,64,128]{3,2,1,0:T(8,128)(2,1)S(1)}, u32[]{:S(2)}, u32[]{:S(2)}) collective-permute-start(bf16[2,2,64,128]{3,2,1,0:T(8,128)(2,1)S(1)} %get-tuple-element.31), channel_id=1, source_target_pairs={{2,0},{3,1},{0,2},{1,3},{6,4},{7,5},{4,6},{5,7},{10,8},{11,9},{8,1... | collective-permute-start | bytes 196616 | tf_op jit(solution)/shard_map/ppermute | solution.py:26
  21.9 0.0 collective-permute-start.7
  21.9 3.8 %collective-permute-start.2 = (bf16[1,2,64,128]{3,2,1,0:T(8,128)(2,1)S(1)}, bf16[1,2,64,128]{3,2,1,0:T(8,128)(2,1)S(1)}, u32[]{:S(2)}, u32[]{:S(2)}) collective-permute-start(bf16[1,2,64,128]{3,2,1,0:T(8,128)(2,1)S(1)} %get-tuple-element.25), channel_id=1, source_target_pairs={{3,0},{2,1},{1,2},{0,3},{7,4},{6,5},{5,6},{4,7},{11,8},{10,9},{9,1... | collective-permute-start | bytes 98312 | tf_op jit(solution)/shard_map/ppermute | solution.py:26
  25.7 2.6 %collective-permute-done.2.refs_3_ = bf16[1,2,64,128]{3,2,1,0:T(8,128)(2,1)S(1)} collective-permute-done((bf16[1,2,64,128]{3,2,1,0:T(8,128)(2,1)S(1)}, bf16[1,2,64,128]{3,2,1,0:T(8,128)(2,1)S(1)}, u32[]{:S(2)}, u32[]{:S(2)}) %collective-permute-start.2) | collective-permute-done | bytes 32800 | tf_op jit(solution)/shard_map/ppermute | solution.py:26
  28.3 0.9 %join.1 = (f32[16,64,64]{2,1,0:T(8,128)}, f32[2,64,128]{2,1,0:T(8,128)S(1)}) custom-call(f32[1,2,64,128]{3,2,1,0:T(8,128)S(1)} %get-tuple-element.22.refs_0_, bf16[1,2,64,128]{3,2,1,0:T(8,128)(2,1)S(1)} %collective-permute-done.refs_1_, bf16[1,2,64,128]{3,2,1,0:T(8,128)(2,1)S(1)} %collective-permute-done.1.refs_2_, ...), custom_call_target="tpu_custom_call" | custom-call | tf_op jit(solution)/shard_map/join/pallas_call | solution.py:217
  29.2 0.1 copy.11
  29.3 1.0 %shard_map.56 = (f32[1,2,64,128]{3,2,1,0:T(8,128)S(1)}, bf16[1,2,64,128]{3,2,1,0:T(8,128)(2,1)S(1)}, bf16[1,2,64,128]{3,2,1,0:T(8,128)(2,1)S(1)}, bf16[1,2,64,128]{3,2,1,0:T(8,128)(2,1)S(1)}) custom-call(bf16[512,3072]{1,0:T(8,128)(2,1)S(1)} %get-tuple-element.26.refs_0_, bf16[64,3072]{1,0:T(8,128)(2,1)S(1)} %bitcast.12), custom_call_target="tpu_custom_call" | custom-call | tf_op jit(solution)/shard_map/pallas_call | solution.py:180
  30.3 1.9 %collective-permute-start.10 = (bf16[1,2,64,128]{3,2,1,0:T(8,128)(2,1)S(1)}, bf16[1,2,64,128]{3,2,1,0:T(8,128)(2,1)S(1)}, u32[]{:S(2)}, u32[]{:S(2)}) collective-permute-start(bf16[1,2,64,128]{3,2,1,0:T(8,128)(2,1)S(1)} %get-tuple-element.35), channel_id=1, source_target_pairs={{1,0},{0,1},{3,2},{2,3},{5,4},{4,5},{7,6},{6,7},{9,8},{8,9},{11,10... | collective-permute-start | bytes 98312 | tf_op jit(solution)/shard_map/ppermute | solution.py:26
  32.2 1.9 %collective-permute-start.11 = (bf16[1,2,64,128]{3,2,1,0:T(8,128)(2,1)S(1)}, bf16[1,2,64,128]{3,2,1,0:T(8,128)(2,1)S(1)}, u32[]{:S(2)}, u32[]{:S(2)}) collective-permute-start(bf16[1,2,64,128]{3,2,1,0:T(8,128)(2,1)S(1)} %get-tuple-element.36), channel_id=1, source_target_pairs={{2,0},{3,1},{0,2},{1,3},{6,4},{7,5},{4,6},{5,7},{10,8},{11,9},{8,1... | collective-permute-start | bytes 98312 | tf_op jit(solution)/shard_map/ppermute | solution.py:26
  34.2 0.6 %collective-permute-start.12 = (bf16[1,2,64,128]{3,2,1,0:T(8,128)(2,1)S(1)}, bf16[1,2,64,128]{3,2,1,0:T(8,128)(2,1)S(1)}, u32[]{:S(2)}, u32[]{:S(2)}) collective-permute-start(bf16[1,2,64,128]{3,2,1,0:T(8,128)(2,1)S(1)} %get-tuple-element.37), channel_id=1, source_target_pairs={{3,0},{2,1},{1,2},{0,3},{7,4},{6,5},{5,6},{4,7},{11,8},{10,9},{9,1... | collective-permute-start | bytes 98312 | tf_op jit(solution)/shard_map/ppermute | solution.py:26
  34.8 2.9 %collective-permute-done.11.refs_2_ = bf16[1,2,64,128]{3,2,1,0:T(8,128)(2,1)S(1)} collective-permute-done((bf16[1,2,64,128]{3,2,1,0:T(8,128)(2,1)S(1)}, bf16[1,2,64,128]{3,2,1,0:T(8,128)(2,1)S(1)}, u32[]{:S(2)}, u32[]{:S(2)}) %collective-permute-start.11) | collective-permute-done | bytes 32800 | tf_op jit(solution)/shard_map/ppermute | solution.py:26
  37.6 2.3 %collective-permute-done.12.refs_3_ = bf16[1,2,64,128]{3,2,1,0:T(8,128)(2,1)S(1)} collective-permute-done((bf16[1,2,64,128]{3,2,1,0:T(8,128)(2,1)S(1)}, bf16[1,2,64,128]{3,2,1,0:T(8,128)(2,1)S(1)}, u32[]{:S(2)}, u32[]{:S(2)}) %collective-permute-start.12) | collective-permute-done | bytes 32800 | tf_op jit(solution)/shard_map/ppermute | solution.py:26
  39.9 0.8 %last.1 = f32[16,64,64]{2,1,0:T(8,128)} custom-call(f32[2,64,128]{2,1,0:T(8,128)S(1)} %collective-permute-done.8.swapped, f32[1,2,64,128]{3,2,1,0:T(8,128)S(1)} %get-tuple-element.34.refs_0_, bf16[1,2,64,128]{3,2,1,0:T(8,128)(2,1)S(1)} %collective-permute-done.10.refs_1_, ...), custom_call_target="tpu_custom_call", output_to_operand_aliasing={{}: (5, {})} | custom-call | tf_op jit(solution)/shard_map/last/pallas_call | solution.py:226
  (10 shorter events, 0.0 us)
Async XLA Ops:
  0.0 12.5 %collective-permute-start.4 = (bf16[64,24,128]{2,1,0:T(8,128)(2,1)}, bf16[64,24,128]{2,1,0:T(8,128)(2,1)S(1)}, u32[]{:S(2)}, u32[]{:S(2)}) collective-permute-start(bf16[64,24,128]{2,1,0:T(8,128)(2,1)} %right.1), channel_id=1, source_target_pairs={{28,0},{24,4},{4,8},{0,12},{12,16},{8,20},{20,24},{16,28},{29,1},{... | collective-permute-start | bytes 1179656 | tf_op jit(solution)/shard_map/ppermute | solution.py:26
  2.4 10.1 %collective-permute-start.3 = (bf16[64,24,128]{2,1,0:T(8,128)(2,1)}, bf16[64,24,128]{2,1,0:T(8,128)(2,1)S(1)}, u32[]{:S(2)}, u32[]{:S(2)}) collective-permute-start(bf16[64,24,128]{2,1,0:T(8,128)(2,1)} %left.1), channel_id=1, source_target_pairs={{4,0},{0,4},{12,8},{8,12},{20,16},{16,20},{28,24},{24,28},{5,1},{1... | collective-permute-start | bytes 1179656 | tf_op jit(solution)/shard_map/ppermute | solution.py:26
  3.1 26.1 %collective-permute-start.9 = (bf16[64,24,128]{2,1,0:T(8,128)(2,1)}, bf16[64,24,128]{2,1,0:T(8,128)(2,1)S(1)}, u32[]{:S(2)}, u32[]{:S(2)}) collective-permute-start(bf16[64,24,128]{2,1,0:T(8,128)(2,1)} %right.1), channel_id=1, source_target_pairs={{20,0},{0,4},{28,8},{8,12},{4,16},{16,20},{12,24},{24,28},{21,1},{... | collective-permute-start | bytes 1179656 | tf_op jit(solution)/shard_map/ppermute | solution.py:26
  6.3 15.6 %collective-permute-start = (bf16[1,2,64,128]{3,2,1,0:T(8,128)(2,1)S(1)}, bf16[1,2,64,128]{3,2,1,0:T(8,128)(2,1)S(1)}, u32[]{:S(2)}, u32[]{:S(2)}) collective-permute-start(bf16[1,2,64,128]{3,2,1,0:T(8,128)(2,1)S(1)} %get-tuple-element.23), channel_id=1, source_target_pairs={{1,0},{0,1},{3,2},{2,3},{5,4},{4,5},{7,6},{6,7},{9,8},{8,9},{11,10... | collective-permute-start | bytes 98312 | tf_op jit(solution)/shard_map/ppermute | solution.py:26
  7.9 14.0 %collective-permute-start.1 = (bf16[1,2,64,128]{3,2,1,0:T(8,128)(2,1)S(1)}, bf16[1,2,64,128]{3,2,1,0:T(8,128)(2,1)S(1)}, u32[]{:S(2)}, u32[]{:S(2)}) collective-permute-start(bf16[1,2,64,128]{3,2,1,0:T(8,128)(2,1)S(1)} %get-tuple-element.24), channel_id=1, source_target_pairs={{2,0},{3,1},{0,2},{1,3},{6,4},{7,5},{4,6},{5,7},{10,8},{11,9},{8,1... | collective-permute-start | bytes 98312 | tf_op jit(solution)/shard_map/ppermute | solution.py:26
  16.1 12.2 %collective-permute-start.5 = (bf16[2,2,64,128]{3,2,1,0:T(8,128)(2,1)S(1)}, bf16[2,2,64,128]{3,2,1,0:T(8,128)(2,1)S(1)}, u32[]{:S(2)}, u32[]{:S(2)}) collective-permute-start(bf16[2,2,64,128]{3,2,1,0:T(8,128)(2,1)S(1)} %get-tuple-element.30), channel_id=1, source_target_pairs={{1,0},{0,1},{3,2},{2,3},{5,4},{4,5},{7,6},{6,7},{9,8},{8,9},{11,10... | collective-permute-start | bytes 196616 | tf_op jit(solution)/shard_map/ppermute | solution.py:26
  19.3 9.0 %collective-permute-start.6 = (bf16[2,2,64,128]{3,2,1,0:T(8,128)(2,1)S(1)}, bf16[2,2,64,128]{3,2,1,0:T(8,128)(2,1)S(1)}, u32[]{:S(2)}, u32[]{:S(2)}) collective-permute-start(bf16[2,2,64,128]{3,2,1,0:T(8,128)(2,1)S(1)} %get-tuple-element.31), channel_id=1, source_target_pairs={{2,0},{3,1},{0,2},{1,3},{6,4},{7,5},{4,6},{5,7},{10,8},{11,9},{8,1... | collective-permute-start | bytes 196616 | tf_op jit(solution)/shard_map/ppermute | solution.py:26
  21.9 6.4 %collective-permute-start.7 = (bf16[2,2,64,128]{3,2,1,0:T(8,128)(2,1)S(1)}, bf16[2,2,64,128]{3,2,1,0:T(8,128)(2,1)S(1)}, u32[]{:S(2)}, u32[]{:S(2)}) collective-permute-start(bf16[2,2,64,128]{3,2,1,0:T(8,128)(2,1)S(1)} %get-tuple-element.32), channel_id=1, source_target_pairs={{3,0},{2,1},{1,2},{0,3},{7,4},{6,5},{5,6},{4,7},{11,8},{10,9},{9,1... | collective-permute-start | bytes 196616 | tf_op jit(solution)/shard_map/ppermute | solution.py:26
  21.9 6.4 %collective-permute-start.2 = (bf16[1,2,64,128]{3,2,1,0:T(8,128)(2,1)S(1)}, bf16[1,2,64,128]{3,2,1,0:T(8,128)(2,1)S(1)}, u32[]{:S(2)}, u32[]{:S(2)}) collective-permute-start(bf16[1,2,64,128]{3,2,1,0:T(8,128)(2,1)S(1)} %get-tuple-element.25), channel_id=1, source_target_pairs={{3,0},{2,1},{1,2},{0,3},{7,4},{6,5},{5,6},{4,7},{11,8},{10,9},{9,1... | collective-permute-start | bytes 98312 | tf_op jit(solution)/shard_map/ppermute | solution.py:26
  29.2 10.7 %collective-permute-start.8 = (f32[2,64,128]{2,1,0:T(8,128)S(1)}, f32[2,64,128]{2,1,0:T(8,128)S(1)}, u32[]{:S(2)}, u32[]{:S(2)}) collective-permute-start(f32[2,64,128]{2,1,0:T(8,128)S(1)} %get-tuple-element.33), channel_id=1, source_target_pairs={{4,0},{0,4},{12,8},{8,12},{20,16},{16,20},{28,24},{24,28},{5,1},{1... | collective-permute-start | bytes 196616 | tf_op jit(solution)/shard_map/ppermute | solution.py:26
  30.3 4.5 %collective-permute-start.10 = (bf16[1,2,64,128]{3,2,1,0:T(8,128)(2,1)S(1)}, bf16[1,2,64,128]{3,2,1,0:T(8,128)(2,1)S(1)}, u32[]{:S(2)}, u32[]{:S(2)}) collective-permute-start(bf16[1,2,64,128]{3,2,1,0:T(8,128)(2,1)S(1)} %get-tuple-element.35), channel_id=1, source_target_pairs={{1,0},{0,1},{3,2},{2,3},{5,4},{4,5},{7,6},{6,7},{9,8},{8,9},{11,10... | collective-permute-start | bytes 98312 | tf_op jit(solution)/shard_map/ppermute | solution.py:26
  32.2 5.4 %collective-permute-start.11 = (bf16[1,2,64,128]{3,2,1,0:T(8,128)(2,1)S(1)}, bf16[1,2,64,128]{3,2,1,0:T(8,128)(2,1)S(1)}, u32[]{:S(2)}, u32[]{:S(2)}) collective-permute-start(bf16[1,2,64,128]{3,2,1,0:T(8,128)(2,1)S(1)} %get-tuple-element.36), channel_id=1, source_target_pairs={{2,0},{3,1},{0,2},{1,3},{6,4},{7,5},{4,6},{5,7},{10,8},{11,9},{8,1... | collective-permute-start | bytes 98312 | tf_op jit(solution)/shard_map/ppermute | solution.py:26
  34.2 5.7 %collective-permute-start.12 = (bf16[1,2,64,128]{3,2,1,0:T(8,128)(2,1)S(1)}, bf16[1,2,64,128]{3,2,1,0:T(8,128)(2,1)S(1)}, u32[]{:S(2)}, u32[]{:S(2)}) collective-permute-start(bf16[1,2,64,128]{3,2,1,0:T(8,128)(2,1)S(1)} %get-tuple-element.37), channel_id=1, source_target_pairs={{3,0},{2,1},{1,2},{0,3},{7,4},{6,5},{5,6},{4,7},{11,8},{10,9},{9,1... | collective-permute-start | bytes 98312 | tf_op jit(solution)/shard_map/ppermute | solution.py:26

commit v4 on v3

--- a/solution.py
+++ b/solution.py
@@ -27,38 +27,47 @@
 
 
 def turn_tables(momenta, phase, angle, cosine, sine):
+    structs = momenta.shape[1]
     sites = angle.shape[1]
     site = lax.axis_index("space") * sites + lax.broadcasted_iota(jnp.int32, (1, sites), 1)
     x = (site % BOX).astype(F32)
     y = (site // BOX % BOX).astype(F32)
     z = (site // (BOX * BOX)).astype(F32)
-    for g in range(momenta.shape[1]):
+    for g in range(structs):
         dot = momenta[0, g].astype(F32) * x + momenta[1, g].astype(F32) * y + momenta[2, g].astype(F32) * z
         for a in range(4):
             angle[g * 4 + a : g * 4 + a + 1, :] = (LAT // 4 * phase[a, g]).astype(F32) - dot
-    steps = angle[...]
+    steps = angle[0 : 4 * structs, :]
     steps = steps - LAT * jnp.floor(steps * (1.0 / LAT))
     psi = steps * (2.0 * math.pi / LAT)
-    cosine[...] = jnp.cos(psi)
-    sine[...] = jnp.sin(psi)
-
-
-def turn_rows(left, perm, cosine, sine, rows):
+    for values, table in ((jnp.cos(psi), cosine), (jnp.sin(psi), sine)):
+        angle[0 : 4 * structs, :] = values
+        for g in range(0, structs, 2):
+            for a in range(4):
+                pair = [jnp.broadcast_to(angle[h * 4 + a : h * 4 + a + 1, :], (sites // 2, sites)) for h in (g, g + 1)]
+                table[g * 2 + a] = jnp.concatenate(pair, axis=0).T
+
+
+def turn_rows(left, perm, cosine, sine, rows, turned, piece=32):
     modes = left.shape[0]
     sites = cosine.shape[1]
     half = 12 * sites
     for a in range(4):
         for k in range(3):
-            at = (a * 3 + k) * sites
-            re = left[:, at : at + sites].astype(F32)
-            im = left[:, half + at : half + at + sites].astype(F32)
-            for g in range(perm.shape[1]):
-                co = cosine[g * 4 + a : g * 4 + a + 1, :]
-                si = sine[g * 4 + a : g * 4 + a + 1, :]
-                to = pl.multiple_of((perm[a, g] * 3 + k) * sites, LANES)
-                rows[g * modes : (g + 1) * modes, pl.ds(to, sites)] = (re * co + im * si).astype(BF16)
-                to = pl.multiple_of(half + (perm[a, g] * 3 + k) * sites, LANES)
-                rows[g * modes : (g + 1) * modes, pl.ds(to, sites)] = (im * co - re * si).astype(BF16)
+            for part in range(2):
+                at = part * half + (a * 3 + k) * sites
+                value = left[:, at : at + sites].astype(F32)
+                turned[part] = jnp.concatenate([value, value], axis=0).T
+            for n in range(0, sites, piece):
+                re, im = turned[0, n : n + piece], turned[1, n : n + piece]
+                for g in range(0, perm.shape[1], 2):
+                    co, si = cosine[g * 2 + a, n : n + piece], sine[g * 2 + a, n : n + piece]
+                    for base, value in ((0, re * co + im * si), (half, im * co - re * si)):
+                        value = value.astype(BF16)
+                        for h in range(2):
+                            to = pl.multiple_of(base + n + (perm[a, g + h] * 3 + k) * sites, piece)
+                            columns = pl.ds((g + h) * modes, modes)
+                            rows[pl.ds(to, piece), columns] = value[:, h * modes : (h + 1) * modes]
 
 
 def flatten(block, flat):
@@ -73,38 +82,41 @@
     both[modes:, 0:half] = right[:, half:]
     both[modes:, half:] = -right[:, 0:half]
     me = lax.axis_index("space")
-    own = kept.shape[1]
+    wide = kept.shape[2]
+
+    def columns(space):
+        return pl.ds(pl.multiple_of(space * wide, LANES), wide)
+
     for slot, rows in enumerate(all_rows):
-        total[...] = lax.dot_general(
-            rows[...], both[...], (((1,), (1,)), ((), ())), preferred_element_type=F32
-        ).reshape(total.shape)
-        kept[slot] = total[pl.ds(me * own, own)]
+        total[...] = jnp.dot(both[...], rows[...], preferred_element_type=F32)
+        kept[slot] = total[:, columns(me)]
         for distance, send in enumerate(sends, 1):
-            send[slot] = total[pl.ds((me ^ distance) * own, own)].astype(BF16)
+            send[slot] = total[:, columns(me ^ distance)].astype(BF16)
 
 
 def first_kernel(n_send, left, right, momenta, perm, phase, rows, cosine, sine, kept, *rest):
-    sends, (both, total, angle, lefts, rights, flat, *tables, done) = rest[:n_send], rest[n_send:]
+    sends, (both, total, angle, lefts, rights, flat, turned, *tables, done) = rest[:n_send], rest[n_send:]
     pairs = list(zip((momenta, perm, phase, left, right), (*tables, lefts, rights)))
     copies = [pltpu.make_async_copy(source, target, done.at[i]) for i, (source, target) in enumerate(pairs)]
     for copy in copies:
         copy.start()
-    for copy in copies[:-1]:
+    for copy in copies[:3]:
         copy.wait()
     turn_tables(tables[0], tables[2], angle, cosine, sine)
+    copies[3].wait()
     flatten(lefts, flat)
-    turn_rows(flat, tables[1], cosine, sine, rows)
-    copies[-1].wait()
+    turn_rows(flat, tables[1], cosine, sine, rows, turned)
+    copies[4].wait()
     flatten(rights, flat)
     multiply((rows,), flat, both, total, kept, sends)
 
 
-def other_kernel(left, perm, cosine, sine, rows, flat, table, done):
+def other_kernel(left, perm, cosine, sine, rows, flat, turned, table, done):
     copy = pltpu.make_async_copy(perm, table, done)
     copy.start()
     flatten(left, flat)
     copy.wait()
-    turn_rows(flat, table, cosine, sine, rows)
+    turn_rows(flat, table, cosine, sine, rows, turned)
 
 
 def product_kernel(n_rows, *refs):
@@ -112,35 +124,38 @@
     multiply(all_rows, right, both, total, kept, sends)
 
 
-def summed(parts, slot, g, factor):
-    value = parts[0][slot, g]
+def summed(parts, slot):
+    value = parts[0][slot]
     for part in parts[1:]:
-        value = value + part[slot, g].astype(F32)
-    return value * factor
+        value = value + part[slot].astype(F32)
+    return value
+
+
+def planes_of(value, factor, modes):
+    turned = (value * factor).T
+    halves = range(0, value.shape[0], modes)
+    return [[turned[g : g + modes, p : p + modes] for p in halves] for g in range(0, value.shape[1], modes)]
 
 
 def join_kernel(spaces, factor, *refs):
     early, middle, (out, other) = refs[:spaces], refs[spaces : 2 * spaces], refs[2 * spaces :]
     odd = lax.axis_index("mode") % 2
-    modes = out.shape[1]
-    for g in range(other.shape[0]):
-        other[g] = summed(middle, 1, g, factor)
-        for parts, place in ((early, 0), (middle, 1 + 2 * odd)):
-            value = summed(parts, 0, g, factor)
+    other[...] = summed(middle, 1)
+    for parts, place in ((early, 0), (middle, 1 + 2 * odd)):
+        for g, pair in enumerate(planes_of(summed(parts, 0), factor, out.shape[1])):
             for p in range(2):
-                out[(g * CYCLE + place) * 2 + p] = value[:, p * modes : (p + 1) * modes]
+                out[(g * CYCLE + place) * 2 + p] = pair[p]
 
 
 def last_kernel(factor, swapped, *refs):
     late, (_, out, planes, done) = refs[:-4], refs[-4:]
     odd = lax.axis_index("mode") % 2
-    modes = out.shape[1]
     copies = []
-    for g in range(swapped.shape[0]):
-        for n, place in enumerate((2, 3 - 2 * odd)):
-            value = swapped[g] if n == 0 else summed(late, 0, g, factor)
+    for n, place in enumerate((2, 3 - 2 * odd)):
+        value = swapped[...] if n == 0 else summed(late, 0)
+        for g, pair in enumerate(planes_of(value, factor, out.shape[1])):
             for p in range(2):
-                planes[g, n, p] = value[:, p * modes : (p + 1) * modes]
+                planes[g, n, p] = pair[p]
             to = out.at[pl.ds((g * CYCLE + place) * 2, 2)]
             copies.append(pltpu.make_async_copy(planes.at[g, n], to, done.at[2 * g + n]))
             copies[-1].start()
@@ -157,10 +172,10 @@
     shape = jax.ShapeDtypeStruct
 
     def outs(slots):
-        size = (slots, own, modes, 2 * modes)
+        size = (slots, 2 * modes, own * modes)
         return [shape(size, F32)] + [shape(size, BF16)] * n_send
 
-    work = [pltpu.VMEM((2 * modes, depth), BF16), pltpu.VMEM((STRUCTS, modes, 2 * modes), F32)]
+    work = [pltpu.VMEM((2 * modes, depth), BF16), pltpu.VMEM((2 * modes, STRUCTS * modes), F32)]
 
     ahead = routed(right_modes, "mode", lambda i: i - 1 if i % 2 == 0 else i - 3)
     other_left = routed(left_modes, "mode", lambda i: i ^ 1)
@@ -169,8 +184,9 @@
     tables = [pltpu.with_memory_space_constraint(t.T, pltpu.HBM) for t in (momenta, spin_perm, spin_phase)]
     table_shapes = [pltpu.SMEM(t.shape, jnp.int32) for t in tables]
     flat = pltpu.VMEM((modes, depth), BF16)
-    rows_shape = shape((STRUCTS * modes, depth), BF16)
-    turn_shape = shape((4 * STRUCTS, sites), F32)
+    turned = pltpu.VMEM((2, sites, 2 * modes), F32)
+    rows_shape = shape((depth, STRUCTS * modes), BF16)
+    turn_shape = shape((2 * STRUCTS, sites, 2 * modes), F32)
 
     def exchange(group):
         kept, *sends = group
@@ -192,9 +208,9 @@
         in_specs=[HBM] * 5,
         out_specs=[VMEM] * (3 + spaces),
         scratch_shapes=work
-        + [pltpu.VMEM(turn_shape.shape, F32)]
+        + [pltpu.VMEM((4 * STRUCTS, sites), F32)]
         + [pltpu.VMEM(left_modes.shape, BF16)] * 2
-        + [flat]
+        + [flat, turned]
         + table_shapes
         + [pltpu.SemaphoreType.DMA((5,))],
         compiler_params=PARAMS,
@@ -206,7 +222,7 @@
         out_shape=rows_shape,
         in_specs=[VMEM, HBM, VMEM, VMEM],
         out_specs=VMEM,
-        scratch_shapes=[flat, table_shapes[1], pltpu.SemaphoreType.DMA],
+        scratch_shapes=[flat, turned, table_shapes[1], pltpu.SemaphoreType.DMA],
         compiler_params=PARAMS,
         name="other",
     )(other_left, tables[1], cosine, sine)
@@ -216,7 +232,7 @@
     result = shape((own * CYCLE * 2, modes, modes), F32)
     out, other = pl.pallas_call(
         functools.partial(join_kernel, spaces, factor),
-        out_shape=[result, shape((own, modes, 2 * modes), F32)],
+        out_shape=[result, shape((2 * modes, own * modes), F32)],
         in_specs=[VMEM] * (2 * spaces),
         out_specs=[VMEM] * 2,
         compiler_params=PARAMS,
@@ -279,10 +295,11 @@
 
 def solution(mesh):
     spaces, n_mode = mesh.shape["space"], mesh.shape["mode"]
-    fits = spaces & (spaces - 1) == 0 and STRUCTS % spaces == 0 and n_mode % 2 == 0 and n_mode >= CYCLE
+    fits = spaces & (spaces - 1) == 0 and STRUCTS % (2 * spaces) == 0 and n_mode % 2 == 0 and n_mode >= CYCLE
 
     def either(left_modes, *rest):
-        body = local if fits and left_modes.shape[2] % LANES == 0 else plain_local
+        square = left_modes.shape[2] == LANES and 2 * left_modes.shape[0] == LANES
+        body = local if fits and square else plain_local
         return body(left_modes, *rest)
 
     placed = (P("mode", None, "space"), P("mode", None, "space"), P(), P(), P())

time: 40.9 us -> 40.1 us (0.980)
  Pallas kernels: 9.47 us -> 9.06 us
    pallas_call x2, Pallas kernels: 2.82 us -> 1.75 us  [product(): pl.pallas_call(functools.partial(product_kernel, len(all_rows)), out_shap...]
  transfers between devices with their start and end apart: 13 -> 13, of which waited for: 4 -> 4; matrix products, arithmetic and copies ran while one was open for 0% -> 0% of each run, Pallas kernels for 21% -> 20%
where the time goes in v4:
time: 40.1 us; the launch traced here: 39.9 us
  starting transfers between devices  21.3 us (53%)
  waiting for transfers between devices  9.31 us (23%)
  Pallas kernels  9.06 us (23%)
    ppermute x13, starting transfers between devices, routed(): lax.ppermute(block, axis, [(source(i) % size, i) for i in range(size)])  21.3 us
    ppermute x13, waiting for transfers between devices, routed(): lax.ppermute(block, axis, [(source(i) % size, i) for i in range(size)])  9.31 us
    pallas_call x1, Pallas kernels, local(): pl.pallas_call(functools.partial(first_kernel, n_send), out_shape=[rows_s...  3.57 us
    pallas_call x1, Pallas kernels, local(): pl.pallas_call(other_kernel, out_shape=rows_shape, in_specs=[VMEM, HBM, V...  1.88 us
    pallas_call x2, Pallas kernels, product(): pl.pallas_call(functools.partial(product_kernel, len(all_rows)), out_shap...  1.75 us
    pallas_call x1, Pallas kernels, local(): pl.pallas_call(functools.partial(join_kernel, spaces, factor), out_shape=...  0.98 us
    pallas_call x1, Pallas kernels, local(): pl.pallas_call(functools.partial(last_kernel, factor), out_shape=result,...  0.88 us
  transfers between devices with their start and end apart: 13, of which 4 were waited for; matrix products, arithmetic and copies ran while one was open for 0% of the time, Pallas kernels for 20%

profile of v4, /device:TPU:0, one launch (start us, length us, event | category | flops | bytes accessed | tf_op | source)
XLA Modules:
  0.0 39.9 jit_solution(4350560834652805005)
XLA Ops:
  0.0 2.4 %collective-permute-start.4 = (bf16[64,24,128]{2,1,0:T(8,128)(2,1)}, bf16[64,24,128]{2,1,0:T(8,128)(2,1)S(1)}, u32[]{:S(2)}, u32[]{:S(2)}) collective-permute-start(bf16[64,24,128]{2,1,0:T(8,128)(2,1)} %right.1), channel_id=1, source_target_pairs={{28,0},{24,4},{4,8},{0,12},{12,16},{8,20},{20,24},{16,28},{29,1},{... | collective-permute-start | bytes 1179656 | tf_op jit(solution)/shard_map/ppermute | solution.py:26
  2.4 0.7 %collective-permute-start.3 = (bf16[64,24,128]{2,1,0:T(8,128)(2,1)}, bf16[64,24,128]{2,1,0:T(8,128)(2,1)S(1)}, u32[]{:S(2)}, u32[]{:S(2)}) collective-permute-start(bf16[64,24,128]{2,1,0:T(8,128)(2,1)} %left.1), channel_id=1, source_target_pairs={{4,0},{0,4},{12,8},{8,12},{20,16},{16,20},{28,24},{24,28},{5,1},{1... | collective-permute-start | bytes 1179656 | tf_op jit(solution)/shard_map/ppermute | solution.py:26
  3.1 0.0 collective-permute-start.9
  3.1 3.6 %first.1 = (bf16[3072,512]{1,0:T(8,128)(2,1)S(1)}, f32[16,128,128]{2,1,0:T(8,128)S(1)}, f32[16,128,128]{2,1,0:T(8,128)S(1)}, f32[1,128,128]{2,1,0:T(8,128)S(1)},...) custom-call(bf16[64,24,128]{2,1,0:T(8,128)(2,1)} %left.1, ...), custom_call_target="tpu_custom_call" | custom-call | tf_op jit(solution)/shard_map/first/pallas_call | solution.py:205
  6.7 1.6 %collective-permute-start = (bf16[1,128,128]{2,1,0:T(8,128)(2,1)S(1)}, bf16[1,128,128]{2,1,0:T(8,128)(2,1)S(1)}, u32[]{:S(2)}, u32[]{:S(2)}) collective-permute-start(bf16[1,128,128]{2,1,0:T(8,128)(2,1)S(1)} %get-tuple-element.23), channel_id=1, source_target_pairs={{1,0},{0,1},{3,2},{2,3},{5,4},{4,5},{7,6},{6,7},{9,8},{8,9},{11,10... | collective-permute-start | bytes 98312 | tf_op jit(solution)/shard_map/ppermute | solution.py:26
  8.3 2.6 %collective-permute-start.1 = (bf16[1,128,128]{2,1,0:T(8,128)(2,1)S(1)}, bf16[1,128,128]{2,1,0:T(8,128)(2,1)S(1)}, u32[]{:S(2)}, u32[]{:S(2)}) collective-permute-start(bf16[1,128,128]{2,1,0:T(8,128)(2,1)S(1)} %get-tuple-element.24), channel_id=1, source_target_pairs={{2,0},{3,1},{0,2},{1,3},{6,4},{7,5},{4,6},{5,7},{10,8},{11,9},{8,1... | collective-permute-start | bytes 98312 | tf_op jit(solution)/shard_map/ppermute | solution.py:26
  10.9 1.6 %collective-permute-done.4 = bf16[64,24,128]{2,1,0:T(8,128)(2,1)S(1)} collective-permute-done((bf16[64,24,128]{2,1,0:T(8,128)(2,1)}, bf16[64,24,128]{2,1,0:T(8,128)(2,1)S(1)}, u32[]{:S(2)}, u32[]{:S(2)}) %collective-permute-start.4) | collective-permute-done | bytes 393248 | tf_op jit(solution)/shard_map/ppermute | solution.py:26
  12.5 0.1 copy.12
  12.6 1.9 %other.1.refs_1_ = bf16[3072,512]{1,0:T(8,128)(2,1)S(1)} custom-call(bf16[64,24,128]{2,1,0:T(8,128)(2,1)S(1)} %collective-permute-done.3.left, s32[4,8]{1,0:T(4,128)} %bitcast.16, f32[16,128,128]{2,1,0:T(8,128)S(1)} %get-tuple-element.27.cosine, f32[16,128,128]{2,1,0:T(8,128)S(1)} %get-tuple-element.28.sine), custom_call_target="tpu_custom_call" | custom-call | tf_op jit(solution)/shard_map/other/pallas_call | solution.py:220
  14.4 1.1 %shard_map.55 = (f32[2,128,128]{2,1,0:T(8,128)S(1)}, bf16[2,128,128]{2,1,0:T(8,128)(2,1)S(1)}, bf16[2,128,128]{2,1,0:T(8,128)(2,1)S(1)}, bf16[2,128,128]{2,1,0:T(8,128)(2,1)S(1)}) custom-call(bf16[3072,512]{1,0:T(8,128)(2,1)S(1)} %get-tuple-element.26.refs_0_, bf16[3072,512]{1,0:T(8,128)(2,1)S(1)} %other.1.refs_1_, bf16[64,3072]{1,0:T(8,128)(2,1)S(1)} %bitcast.11), custom_call_target="tpu_custom_call" | custom-call | tf_op jit(solution)/shard_map/pallas_call | solution.py:196
  15.6 3.2 %collective-permute-start.5 = (bf16[2,128,128]{2,1,0:T(8,128)(2,1)S(1)}, bf16[2,128,128]{2,1,0:T(8,128)(2,1)S(1)}, u32[]{:S(2)}, u32[]{:S(2)}) collective-permute-start(bf16[2,128,128]{2,1,0:T(8,128)(2,1)S(1)} %get-tuple-element.30), channel_id=1, source_target_pairs={{1,0},{0,1},{3,2},{2,3},{5,4},{4,5},{7,6},{6,7},{9,8},{8,9},{11,10... | collective-permute-start | bytes 196616 | tf_op jit(solution)/shard_map/ppermute | solution.py:26
  18.7 2.6 %collective-permute-start.6 = (bf16[2,128,128]{2,1,0:T(8,128)(2,1)S(1)}, bf16[2,128,128]{2,1,0:T(8,128)(2,1)S(1)}, u32[]{:S(2)}, u32[]{:S(2)}) collective-permute-start(bf16[2,128,128]{2,1,0:T(8,128)(2,1)S(1)} %get-tuple-element.31), channel_id=1, source_target_pairs={{2,0},{3,1},{0,2},{1,3},{6,4},{7,5},{4,6},{5,7},{10,8},{11,9},{8,1... | collective-permute-start | bytes 196616 | tf_op jit(solution)/shard_map/ppermute | solution.py:26
  21.3 0.0 collective-permute-done.refs_1_
  21.3 3.8 %collective-permute-start.2 = (bf16[1,128,128]{2,1,0:T(8,128)(2,1)S(1)}, bf16[1,128,128]{2,1,0:T(8,128)(2,1)S(1)}, u32[]{:S(2)}, u32[]{:S(2)}) collective-permute-start(bf16[1,128,128]{2,1,0:T(8,128)(2,1)S(1)} %get-tuple-element.25), channel_id=1, source_target_pairs={{3,0},{2,1},{1,2},{0,3},{7,4},{6,5},{5,6},{4,7},{11,8},{10,9},{9,1... | collective-permute-start | bytes 98312 | tf_op jit(solution)/shard_map/ppermute | solution.py:26
  25.1 2.6 %collective-permute-done.2.refs_3_ = bf16[1,128,128]{2,1,0:T(8,128)(2,1)S(1)} collective-permute-done((bf16[1,128,128]{2,1,0:T(8,128)(2,1)S(1)}, bf16[1,128,128]{2,1,0:T(8,128)(2,1)S(1)}, u32[]{:S(2)}, u32[]{:S(2)}) %collective-permute-start.2) | collective-permute-done | bytes 32800 | tf_op jit(solution)/shard_map/ppermute | solution.py:26
  27.7 1.0 %join.1 = (f32[16,64,64]{2,1,0:T(8,128)}, f32[128,128]{1,0:T(8,128)S(1)}) custom-call(f32[1,128,128]{2,1,0:T(8,128)S(1)} %get-tuple-element.22.refs_0_, bf16[1,128,128]{2,1,0:T(8,128)(2,1)S(1)} %collective-permute-done.refs_1_, bf16[1,128,128]{2,1,0:T(8,128)(2,1)S(1)} %collective-permute-done.1.refs_2_, ...), custom_call_target="tpu_custom_call" | custom-call | tf_op jit(solution)/shard_map/join/pallas_call | solution.py:233
  28.7 0.1 copy.11
  28.8 0.6 %shard_map.56 = (f32[1,128,128]{2,1,0:T(8,128)S(1)}, bf16[1,128,128]{2,1,0:T(8,128)(2,1)S(1)}, bf16[1,128,128]{2,1,0:T(8,128)(2,1)S(1)}, bf16[1,128,128]{2,1,0:T(8,128)(2,1)S(1)}) custom-call(bf16[3072,512]{1,0:T(8,128)(2,1)S(1)} %get-tuple-element.26.refs_0_, bf16[64,3072]{1,0:T(8,128)(2,1)S(1)} %bitcast.12), custom_call_target="tpu_custom_call" | custom-call | tf_op jit(solution)/shard_map/pallas_call | solution.py:196
  29.4 2.0 %collective-permute-start.10 = (bf16[1,128,128]{2,1,0:T(8,128)(2,1)S(1)}, bf16[1,128,128]{2,1,0:T(8,128)(2,1)S(1)}, u32[]{:S(2)}, u32[]{:S(2)}) collective-permute-start(bf16[1,128,128]{2,1,0:T(8,128)(2,1)S(1)} %get-tuple-element.35), channel_id=1, source_target_pairs={{1,0},{0,1},{3,2},{2,3},{5,4},{4,5},{7,6},{6,7},{9,8},{8,9},{11,10... | collective-permute-start | bytes 98312 | tf_op jit(solution)/shard_map/ppermute | solution.py:26
  31.4 1.9 %collective-permute-start.11 = (bf16[1,128,128]{2,1,0:T(8,128)(2,1)S(1)}, bf16[1,128,128]{2,1,0:T(8,128)(2,1)S(1)}, u32[]{:S(2)}, u32[]{:S(2)}) collective-permute-start(bf16[1,128,128]{2,1,0:T(8,128)(2,1)S(1)} %get-tuple-element.36), channel_id=1, source_target_pairs={{2,0},{3,1},{0,2},{1,3},{6,4},{7,5},{4,6},{5,7},{10,8},{11,9},{8,1... | collective-permute-start | bytes 98312 | tf_op jit(solution)/shard_map/ppermute | solution.py:26
  33.3 0.6 %collective-permute-start.12 = (bf16[1,128,128]{2,1,0:T(8,128)(2,1)S(1)}, bf16[1,128,128]{2,1,0:T(8,128)(2,1)S(1)}, u32[]{:S(2)}, u32[]{:S(2)}) collective-permute-start(bf16[1,128,128]{2,1,0:T(8,128)(2,1)S(1)} %get-tuple-element.37), channel_id=1, source_target_pairs={{3,0},{2,1},{1,2},{0,3},{7,4},{6,5},{5,6},{4,7},{11,8},{10,9},{9,1... | collective-permute-start | bytes 98312 | tf_op jit(solution)/shard_map/ppermute | solution.py:26
  33.9 2.9 %collective-permute-done.11.refs_2_ = bf16[1,128,128]{2,1,0:T(8,128)(2,1)S(1)} collective-permute-done((bf16[1,128,128]{2,1,0:T(8,128)(2,1)S(1)}, bf16[1,128,128]{2,1,0:T(8,128)(2,1)S(1)}, u32[]{:S(2)}, u32[]{:S(2)}) %collective-permute-start.11) | collective-permute-done | bytes 32800 | tf_op jit(solution)/shard_map/ppermute | solution.py:26
  36.8 2.2 %collective-permute-done.12.refs_3_ = bf16[1,128,128]{2,1,0:T(8,128)(2,1)S(1)} collective-permute-done((bf16[1,128,128]{2,1,0:T(8,128)(2,1)S(1)}, bf16[1,128,128]{2,1,0:T(8,128)(2,1)S(1)}, u32[]{:S(2)}, u32[]{:S(2)}) %collective-permute-start.12) | collective-permute-done | bytes 32800 | tf_op jit(solution)/shard_map/ppermute | solution.py:26
  39.0 0.9 %last.1 = f32[16,64,64]{2,1,0:T(8,128)} custom-call(f32[128,128]{1,0:T(8,128)S(1)} %collective-permute-done.8.swapped, f32[1,128,128]{2,1,0:T(8,128)S(1)} %get-tuple-element.34.refs_0_, bf16[1,128,128]{2,1,0:T(8,128)(2,1)S(1)} %collective-permute-done.10.refs_1_, ...), custom_call_target="tpu_custom_call", output_to_operand_aliasing={{}: (5, {})} | custom-call | tf_op jit(solution)/shard_map/last/pallas_call | solution.py:242
  (10 shorter events, 0.0 us)
Async XLA Ops:
  0.0 12.5 %collective-permute-start.4 = (bf16[64,24,128]{2,1,0:T(8,128)(2,1)}, bf16[64,24,128]{2,1,0:T(8,128)(2,1)S(1)}, u32[]{:S(2)}, u32[]{:S(2)}) collective-permute-start(bf16[64,24,128]{2,1,0:T(8,128)(2,1)} %right.1), channel_id=1, source_target_pairs={{28,0},{24,4},{4,8},{0,12},{12,16},{8,20},{20,24},{16,28},{29,1},{... | collective-permute-start | bytes 1179656 | tf_op jit(solution)/shard_map/ppermute | solution.py:26
  2.4 10.1 %collective-permute-start.3 = (bf16[64,24,128]{2,1,0:T(8,128)(2,1)}, bf16[64,24,128]{2,1,0:T(8,128)(2,1)S(1)}, u32[]{:S(2)}, u32[]{:S(2)}) collective-permute-start(bf16[64,24,128]{2,1,0:T(8,128)(2,1)} %left.1), channel_id=1, source_target_pairs={{4,0},{0,4},{12,8},{8,12},{20,16},{16,20},{28,24},{24,28},{5,1},{1... | collective-permute-start | bytes 1179656 | tf_op jit(solution)/shard_map/ppermute | solution.py:26
  3.1 25.6 %collective-permute-start.9 = (bf16[64,24,128]{2,1,0:T(8,128)(2,1)}, bf16[64,24,128]{2,1,0:T(8,128)(2,1)S(1)}, u32[]{:S(2)}, u32[]{:S(2)}) collective-permute-start(bf16[64,24,128]{2,1,0:T(8,128)(2,1)} %right.1), channel_id=1, source_target_pairs={{20,0},{0,4},{28,8},{8,12},{4,16},{16,20},{12,24},{24,28},{21,1},{... | collective-permute-start | bytes 1179656 | tf_op jit(solution)/shard_map/ppermute | solution.py:26
  6.7 14.7 %collective-permute-start = (bf16[1,128,128]{2,1,0:T(8,128)(2,1)S(1)}, bf16[1,128,128]{2,1,0:T(8,128)(2,1)S(1)}, u32[]{:S(2)}, u32[]{:S(2)}) collective-permute-start(bf16[1,128,128]{2,1,0:T(8,128)(2,1)S(1)} %get-tuple-element.23), channel_id=1, source_target_pairs={{1,0},{0,1},{3,2},{2,3},{5,4},{4,5},{7,6},{6,7},{9,8},{8,9},{11,10... | collective-permute-start | bytes 98312 | tf_op jit(solution)/shard_map/ppermute | solution.py:26
  8.3 13.0 %collective-permute-start.1 = (bf16[1,128,128]{2,1,0:T(8,128)(2,1)S(1)}, bf16[1,128,128]{2,1,0:T(8,128)(2,1)S(1)}, u32[]{:S(2)}, u32[]{:S(2)}) collective-permute-start(bf16[1,128,128]{2,1,0:T(8,128)(2,1)S(1)} %get-tuple-element.24), channel_id=1, source_target_pairs={{2,0},{3,1},{0,2},{1,3},{6,4},{7,5},{4,6},{5,7},{10,8},{11,9},{8,1... | collective-permute-start | bytes 98312 | tf_op jit(solution)/shard_map/ppermute | solution.py:26
  15.6 12.2 %collective-permute-start.5 = (bf16[2,128,128]{2,1,0:T(8,128)(2,1)S(1)}, bf16[2,128,128]{2,1,0:T(8,128)(2,1)S(1)}, u32[]{:S(2)}, u32[]{:S(2)}) collective-permute-start(bf16[2,128,128]{2,1,0:T(8,128)(2,1)S(1)} %get-tuple-element.30), channel_id=1, source_target_pairs={{1,0},{0,1},{3,2},{2,3},{5,4},{4,5},{7,6},{6,7},{9,8},{8,9},{11,10... | collective-permute-start | bytes 196616 | tf_op jit(solution)/shard_map/ppermute | solution.py:26
  18.7 9.0 %collective-permute-start.6 = (bf16[2,128,128]{2,1,0:T(8,128)(2,1)S(1)}, bf16[2,128,128]{2,1,0:T(8,128)(2,1)S(1)}, u32[]{:S(2)}, u32[]{:S(2)}) collective-permute-start(bf16[2,128,128]{2,1,0:T(8,128)(2,1)S(1)} %get-tuple-element.31), channel_id=1, source_target_pairs={{2,0},{3,1},{0,2},{1,3},{6,4},{7,5},{4,6},{5,7},{10,8},{11,9},{8,1... | collective-permute-start | bytes 196616 | tf_op jit(solution)/shard_map/ppermute | solution.py:26
  21.3 6.4 %collective-permute-start.7 = (bf16[2,128,128]{2,1,0:T(8,128)(2,1)S(1)}, bf16[2,128,128]{2,1,0:T(8,128)(2,1)S(1)}, u32[]{:S(2)}, u32[]{:S(2)}) collective-permute-start(bf16[2,128,128]{2,1,0:T(8,128)(2,1)S(1)} %get-tuple-element.32), channel_id=1, source_target_pairs={{3,0},{2,1},{1,2},{0,3},{7,4},{6,5},{5,6},{4,7},{11,8},{10,9},{9,1... | collective-permute-start | bytes 196616 | tf_op jit(solution)/shard_map/ppermute | solution.py:26
  21.3 6.4 %collective-permute-start.2 = (bf16[1,128,128]{2,1,0:T(8,128)(2,1)S(1)}, bf16[1,128,128]{2,1,0:T(8,128)(2,1)S(1)}, u32[]{:S(2)}, u32[]{:S(2)}) collective-permute-start(bf16[1,128,128]{2,1,0:T(8,128)(2,1)S(1)} %get-tuple-element.25), channel_id=1, source_target_pairs={{3,0},{2,1},{1,2},{0,3},{7,4},{6,5},{5,6},{4,7},{11,8},{10,9},{9,1... | collective-permute-start | bytes 98312 | tf_op jit(solution)/shard_map/ppermute | solution.py:26
  28.7 10.3 %collective-permute-start.8 = (f32[128,128]{1,0:T(8,128)S(1)}, f32[128,128]{1,0:T(8,128)S(1)}, u32[]{:S(2)}, u32[]{:S(2)}) collective-permute-start(f32[128,128]{1,0:T(8,128)S(1)} %get-tuple-element.33), channel_id=1, source_target_pairs={{4,0},{0,4},{12,8},{8,12},{20,16},{16,20},{28,24},{24,28},{5,1},{1... | collective-permute-start | bytes 196616 | tf_op jit(solution)/shard_map/ppermute | solution.py:26
  29.4 4.5 %collective-permute-start.10 = (bf16[1,128,128]{2,1,0:T(8,128)(2,1)S(1)}, bf16[1,128,128]{2,1,0:T(8,128)(2,1)S(1)}, u32[]{:S(2)}, u32[]{:S(2)}) collective-permute-start(bf16[1,128,128]{2,1,0:T(8,128)(2,1)S(1)} %get-tuple-element.35), channel_id=1, source_target_pairs={{1,0},{0,1},{3,2},{2,3},{5,4},{4,5},{7,6},{6,7},{9,8},{8,9},{11,10... | collective-permute-start | bytes 98312 | tf_op jit(solution)/shard_map/ppermute | solution.py:26
  31.4 5.4 %collective-permute-start.11 = (bf16[1,128,128]{2,1,0:T(8,128)(2,1)S(1)}, bf16[1,128,128]{2,1,0:T(8,128)(2,1)S(1)}, u32[]{:S(2)}, u32[]{:S(2)}) collective-permute-start(bf16[1,128,128]{2,1,0:T(8,128)(2,1)S(1)} %get-tuple-element.36), channel_id=1, source_target_pairs={{2,0},{3,1},{0,2},{1,3},{6,4},{7,5},{4,6},{5,7},{10,8},{11,9},{8,1... | collective-permute-start | bytes 98312 | tf_op jit(solution)/shard_map/ppermute | solution.py:26
  33.3 5.7 %collective-permute-start.12 = (bf16[1,128,128]{2,1,0:T(8,128)(2,1)S(1)}, bf16[1,128,128]{2,1,0:T(8,128)(2,1)S(1)}, u32[]{:S(2)}, u32[]{:S(2)}) collective-permute-start(bf16[1,128,128]{2,1,0:T(8,128)(2,1)S(1)} %get-tuple-element.37), channel_id=1, source_target_pairs={{3,0},{2,1},{1,2},{0,3},{7,4},{6,5},{5,6},{4,7},{11,8},{10,9},{9,1... | collective-permute-start | bytes 98312 | tf_op jit(solution)/shard_map/ppermute | solution.py:26
